TPU v7x, 256 devices: a whole 4x4x8 slice. The times are simulated.
256 devices in a mesh: sub: 32 (over y, z), crs: 8 (over x, core).
Axes of the slice: x: 4, y: 4, z: 8, core: 2. Of those that a mesh axis runs over, the one named last changes fastest.
Arguments:
- dual_ops: bfloat16 [384, 1536, 1536], P('sub', 'crs')
- rigid_traces: float32 [384, 6, 1536], P('sub'), may hold values from -0.625 to 0.625
- coarse_factor: float32 [2304, 2304], P('sub', 'crs')
- partner: int32 [384, 12], P('sub'), may hold values from -1 to 287, as said below
- send_list: int32 [64, 72], P('sub'), may hold values from -1 to 143, as said below
- mode_count: int32 [384], P('sub'), may hold values from 0 to 6
- dual_rhs: float32 [384, 1536], P('sub'), may hold values from -6 to 6
- rigid_load: float32 [2304], P('sub'), may hold values from -2400 to 2400
Outputs:
- multipliers: float32 [384, 1536], P('sub')
- projected_residual: float32 [384, 1536], P('sub')
Inputs may be any that keep to these rules, and one draw needn't show every extreme that they name: For each block of a subdomain (subdomains in order, 12 blocks each): -1 for a padding block, else the position of its partner block in the list made of this index of sub's 12 * 12 blocks in order, then the 72 blocks received from the index before along sub, then the 72 from the index after. Partnership is mutual, never a block with itself, never across more than one index of sub. `send_list`: rows 2i and 2i+1 belong to index i of sub: its local blocks sent to the index before and to the index after, -1 in unused slots; the k-th block received from a neighbour is the k-th entry of that neighbour's row toward this index. The first index sends nothing before and the last nothing after; each boundary between neighbouring indices carries 72 // 2 to 72 blocks, one boundary exactly 72.
All inputs are finite; a program needn't handle non-finite values.
Results may differ from a plain program's by a relative error of at most 0.012.
The roundings to bfloat16 on the way count: a program that leaves them out, or rounds other values in their place, can miss the bound.
Values sent between devices are 32-bit elements; how exact they have to be, the bound alone decides.
A program may use at most 64 MiB of HBM per device.

v0:
```python
import jax
import jax.numpy as jnp
from jax import lax
from jax.sharding import PartitionSpec as P

ITERATIONS = 2


def with_halo(block, sides, width):
    for axis, dim in sides:
        count = lax.axis_size(axis)
        forward = [(i, i + 1) for i in range(count - 1)]
        backward = [(target, source) for source, target in forward]
        low = lax.ppermute(
            lax.slice_in_dim(block, block.shape[dim] - width, None, axis=dim), axis, forward
        )
        high = lax.ppermute(lax.slice_in_dim(block, 0, width, axis=dim), axis, backward)
        block = jnp.concatenate([low, block, high], axis=dim)
    return block


def in_order(blocks, dim):
    dims = list(blocks.shape[1:])
    dims[dim] *= blocks.shape[0]
    return jnp.moveaxis(blocks, 0, dim).reshape(dims)


def copy_for_each(shard, axis):
    count = lax.axis_size(axis)
    return lax.all_to_all(
        jnp.broadcast_to(shard[None], (count, *shard.shape)), axis, 0, 0, tiled=True
    )


def gathered_copies(shard, axis, dim):
    return in_order(copy_for_each(shard, axis), dim)


def over_copies(shard, axis):
    return copy_for_each(shard, axis).sum(axis=0)


def together(arrays, axis):
    ravelled, at, done = (jnp.concatenate([a.reshape(-1) for a in arrays]), 0, [])
    so_far = over_copies(ravelled, axis)
    for a in arrays:
        done.append(so_far[at : at + a.size].reshape(a.shape))
        at += a.size
    return tuple(done)


def local(
    dual_ops, rigid_traces, coarse_factor, partner, send_list, mode_count, dual_rhs, rigid_load
):
    sub_count = dual_ops.shape[0]
    block_num = partner.shape[1]
    order_len = dual_ops.shape[2]
    block_len = order_len // block_num
    local_blocks = sub_count * block_num
    mode_num = rigid_traces.shape[1]
    links = partner.reshape(local_blocks)
    linked = (links >= 0)[:, None]
    source = jnp.maximum(links, 0)
    sending = (send_list >= 0)[:, :, None]
    picked = jnp.maximum(send_list, 0)
    mode_mask = (jnp.arange(mode_num, dtype=jnp.int32)[None, :] < mode_count[:, None]).astype(
        jnp.float32
    )

    def jump(vector):
        pieces = vector.reshape(local_blocks, block_len)
        parcels = jnp.where(sending, pieces[picked], 0.0)
        arrived = with_halo(parcels, (("sub", 0),), 1)
        incoming = jnp.concatenate([arrived[0], arrived[3]], axis=0)
        gathered = jnp.concatenate([pieces, incoming], axis=0)
        return jnp.where(linked, pieces - gathered[source], 0.0).reshape(vector.shape)

    def operator(vector):
        lowered = jump(vector).astype(jnp.bfloat16)
        partial_rows = jnp.einsum(
            "srk,sk->sr", dual_ops, lowered, preferred_element_type=jnp.float32
        )
        full_rows = gathered_copies(partial_rows, "crs", 1)
        return jump(full_rows)

    def restrict(vector):
        traced = (
            jnp.einsum("skm,sm->sk", rigid_traces, jump(vector), precision=lax.Precision.HIGHEST)
            * mode_mask
        )
        return traced.reshape(sub_count * mode_num)

    def expand(coarse_vec):
        scaled = coarse_vec.reshape(sub_count, mode_num) * mode_mask
        spread = jnp.einsum("skm,sk->sm", rigid_traces, scaled, precision=lax.Precision.HIGHEST)
        return jump(spread)

    def coarse(restricted, squares):
        column_part = jnp.dot(restricted, coarse_factor, precision=lax.Precision.HIGHEST)
        column_sum, total_sq = together((column_part, squares), "sub")
        back_part = jnp.dot(coarse_factor, column_sum, precision=lax.Precision.HIGHEST)
        solved, folded = together((back_part, jnp.sum(column_sum * column_sum)), "crs")
        return (solved, total_sq, folded)

    def project(residual):
        solved, total_sq, folded = coarse(restrict(residual), jnp.sum(residual * residual))
        projected = residual - expand(solved)
        inner_rw = total_sq - folded
        return (projected, inner_rw)

    start_load = rigid_load * mode_mask.reshape(sub_count * mode_num)
    start_solved, unused_sq, unused_fold = coarse(start_load, jnp.zeros((), jnp.float32))
    multipliers = expand(start_solved)
    residual = dual_rhs - operator(multipliers)
    projected, inner_rw = project(residual)
    direction = projected
    for turn_idx in range(ITERATIONS):
        applied = operator(direction)
        curvature = over_copies(jnp.sum(direction * applied), "sub")
        step_len = inner_rw / curvature
        multipliers = multipliers + step_len * direction
        residual = residual - step_len * applied
        projected, next_rw = project(residual)
        direction = projected + next_rw / inner_rw * direction
        inner_rw = next_rw
    return (multipliers, projected)


def solution(mesh):
    return jax.shard_map(
        local,
        mesh=mesh,
        in_specs=(
            P("sub", "crs", None),
            P("sub", None, None),
            P("sub", "crs"),
            P("sub", None),
            P("sub", None),
            P("sub"),
            P("sub", None),
            P("sub"),
        ),
        out_specs=(P("sub", None), P("sub", None)),
        check_vma=False,
    )
```

profile of v0, /device:TPU:1, one launch (start us, length us, event | category | flops | bytes accessed | tf_op | source)
XLA Modules:
  0.0 353.5 jit_solution(3222715099296155614)
XLA Ops:
  0.6 0.8 iota_compare_fusion
  1.5 1.1 convolution_reduce_fusion.3
  3.4 12.0 %all-to-all-start = ((f32[32,1,289]{2,1,0:T(1,128)}), f32[32,1,289]{2,1,0:T(1,128)S(1)}, u32[]{:S(2)}, u32[]{:S(2)}) async-start(f32[32,1,289]{2,1,0:T(1,128)} %broadcast_in_dim.238), calls=%async_computation | async-start | bytes 98304 | tf_op jit(solution)/shard_map/all_to_all | solution.py:30
  18.2 6.0 %all-to-all-done = f32[32,1,289]{2,1,0:T(1,128)S(1)} async-done(((f32[32,1,289]{2,1,0:T(1,128)}), f32[32,1,289]{2,1,0:T(1,128)S(1)}, u32[]{:S(2)}, u32[]{:S(2)}) %all-to-all-start) | async-done | bytes 37024 | tf_op jit(solution)/shard_map/all_to_all | solution.py:30
  24.9 1.1 convolution_bitcast_fusion.3
  27.3 6.4 %all-to-all-start.1 = ((f32[8,1,73]{2,1,0:T(1,128)}), f32[8,1,73]{2,1,0:T(1,128)S(1)}, u32[]{:S(2)}, u32[]{:S(2)}) async-start(f32[8,1,73]{2,1,0:T(1,128)} %broadcast_in_dim.239), calls=%async_computation.1 | async-start | bytes 8192 | tf_op jit(solution)/shard_map/all_to_all | solution.py:30
  33.8 4.4 %all-to-all-done.1 = f32[8,1,73]{2,1,0:T(1,128)S(1)} async-done(((f32[8,1,73]{2,1,0:T(1,128)}), f32[8,1,73]{2,1,0:T(1,128)S(1)}, u32[]{:S(2)}, u32[]{:S(2)}) %all-to-all-start.1) | async-done | bytes 2368 | tf_op jit(solution)/shard_map/all_to_all | solution.py:30
  40.5 2.4 collective-permute-start
  42.9 1.3 collective-permute-start.1
  44.4 3.3 collective-permute-done.1
  49.2 2.3 collective-permute-start.2
  51.5 1.3 collective-permute-start.3
  53.0 3.2 collective-permute-done.3
  57.0 5.0 %fusion.10 = f32[12,1,192]{2,1,0:T(1,128)S(1)} fusion(bf16[12,192,1536]{2,1,0:T(8,128)(2,1)} %param.8, bf16[12,1536,1]{1,0,2:T(8,128)(2,1)S(1)} %fusion.12), kind=kOutput, calls=%fused_computation.82 | convolution fusion | flops 7077888 | bytes 7123968 | tf_op jit(solution)/shard_map/srk,sk->sr/dot_general | solution.py:80
  62.0 11.2 %all_to_all.75 = f32[8,12,192]{2,1,0:T(8,128)S(1)} all-to-all(f32[8,12,192]{2,1,0:T(8,128)S(1)} %broadcast_in_dim.246), channel_id=1, replica_groups=mesh['sub'=32,'crs'=8] {'crs'}, dimensions={0} | all-to-all | bytes 147456 | tf_op jit(solution)/shard_map/all_to_all | solution.py:30
  74.1 2.1 collective-permute-start.4
  76.2 1.3 collective-permute-start.5
  77.6 3.4 collective-permute-done.5
  83.1 3.4 collective-permute-start.6
  86.5 1.3 collective-permute-start.7
  87.8 3.4 collective-permute-done.7
  91.9 1.3 fusion.8
  94.4 20.0 %all_to_all.76 = f32[32,1,289]{2,1,0:T(1,128)S(1)} all-to-all(f32[32,1,289]{2,1,0:T(1,128)S(1)} %broadcast_in_dim.247), channel_id=1, replica_groups=mesh['sub'=32,'crs'=8] {'sub'}, dimensions={0} | all-to-all | bytes 73984 | tf_op jit(solution)/shard_map/all_to_all | solution.py:30
  116.0 11.5 %all_to_all.77 = f32[8,1,73]{2,1,0:T(1,128)S(1)} all-to-all(f32[8,1,73]{2,1,0:T(1,128)S(1)} %broadcast_in_dim.248), channel_id=1, replica_groups=mesh['sub'=32,'crs'=8] {'crs'}, dimensions={0} | all-to-all | bytes 4672 | tf_op jit(solution)/shard_map/all_to_all | solution.py:30
  129.1 2.4 collective-permute-start.8
  131.6 1.3 collective-permute-start.9
  132.9 3.4 collective-permute-done.9
  137.8 2.3 collective-permute-start.10
  140.1 1.3 collective-permute-start.11
  141.4 3.4 collective-permute-done.11
  145.5 4.9 %fusion.6 = f32[12,1,192]{2,1,0:T(1,128)S(1)} fusion(bf16[12,192,1536]{2,1,0:T(8,128)(2,1)} %param.8, bf16[12,1536,1]{1,0,2:T(8,128)(2,1)S(1)} %fusion.13), kind=kOutput, calls=%fused_computation.78 | convolution fusion | flops 7077888 | bytes 7123968 | tf_op jit(solution)/shard_map/srk,sk->sr/dot_general | solution.py:80
  150.5 11.2 %all_to_all.78 = f32[8,12,192]{2,1,0:T(8,128)S(1)} all-to-all(f32[8,12,192]{2,1,0:T(8,128)S(1)} %broadcast_in_dim.249), channel_id=1, replica_groups=mesh['sub'=32,'crs'=8] {'crs'}, dimensions={0} | all-to-all | bytes 147456 | tf_op jit(solution)/shard_map/all_to_all | solution.py:30
  162.6 2.1 collective-permute-start.12
  164.7 1.3 collective-permute-start.13
  166.1 3.4 collective-permute-done.13
  170.8 1.3 broadcast_in_dim.250
  172.1 10.7 %all-to-all-start.6 = ((f32[32,1,1]{2,1,0:T(1,128)}), f32[32,1,1]{2,1,0:T(1,128)S(1)}, u32[]{:S(2)}, u32[]{:S(2)}) async-start(f32[32,1,1]{2,1,0:T(1,128)} %broadcast_in_dim.250), calls=%async_computation.6 | async-start | bytes 32768 | tf_op jit(solution)/shard_map/all_to_all | solution.py:30
  185.4 6.0 %all-to-all-done.6 = f32[32,1,1]{2,1,0:T(1,128)S(1)} async-done(((f32[32,1,1]{2,1,0:T(1,128)}), f32[32,1,1]{2,1,0:T(1,128)S(1)}, u32[]{:S(2)}, u32[]{:S(2)}) %all-to-all-start.6) | async-done | bytes 160 | tf_op jit(solution)/shard_map/all_to_all | solution.py:30
  194.2 2.2 collective-permute-start.14
  196.4 1.3 collective-permute-start.15
  197.7 3.4 collective-permute-done.15
  201.8 1.3 fusion.4
  204.3 16.2 %all_to_all.79 = f32[32,1,289]{2,1,0:T(1,128)S(1)} all-to-all(f32[32,1,289]{2,1,0:T(1,128)S(1)} %broadcast_in_dim.251), channel_id=1, replica_groups=mesh['sub'=32,'crs'=8] {'sub'}, dimensions={0} | all-to-all | bytes 73984 | tf_op jit(solution)/shard_map/all_to_all | solution.py:30
  222.2 13.2 %all_to_all.80 = f32[8,1,73]{2,1,0:T(1,128)S(1)} all-to-all(f32[8,1,73]{2,1,0:T(1,128)S(1)} %broadcast_in_dim.252), channel_id=1, replica_groups=mesh['sub'=32,'crs'=8] {'crs'}, dimensions={0} | all-to-all | bytes 4672 | tf_op jit(solution)/shard_map/all_to_all | solution.py:30
  237.0 2.4 collective-permute-start.16
  239.4 1.3 collective-permute-start.17
  245.7 3.2 collective-permute-start.18
  248.9 1.3 collective-permute-start.19
  250.2 3.4 collective-permute-done.19
  254.3 4.9 %fusion.2 = f32[12,1,192]{2,1,0:T(1,128)S(1)} fusion(bf16[12,192,1536]{2,1,0:T(8,128)(2,1)} %param.8, bf16[12,1536,1]{1,0,2:T(8,128)(2,1)S(1)} %fusion.14), kind=kOutput, calls=%fused_computation.74 | convolution fusion | flops 7077888 | bytes 7123968 | tf_op jit(solution)/shard_map/srk,sk->sr/dot_general | solution.py:80
  259.3 10.3 %all_to_all.81 = f32[8,12,192]{2,1,0:T(8,128)S(1)} all-to-all(f32[8,12,192]{2,1,0:T(8,128)S(1)} %broadcast_in_dim.253), channel_id=1, replica_groups=mesh['sub'=32,'crs'=8] {'crs'}, dimensions={0} | all-to-all | bytes 147456 | tf_op jit(solution)/shard_map/all_to_all | solution.py:30
  270.6 2.3 collective-permute-start.20
  272.8 1.3 collective-permute-start.21
  274.2 3.3 collective-permute-done.21
  279.5 19.8 %all_to_all.82 = f32[32,1,1]{2,1,0:T(1,128)S(1)} all-to-all(f32[32,1,1]{2,1,0:T(1,128)S(1)} %broadcast_in_dim.254), channel_id=1, replica_groups=mesh['sub'=32,'crs'=8] {'sub'}, dimensions={0} | all-to-all | bytes 256 | tf_op jit(solution)/shard_map/all_to_all | solution.py:30
  302.1 2.2 collective-permute-start.22
  304.3 1.3 collective-permute-start.23
  305.6 3.4 collective-permute-done.23
  309.7 1.3 fusion
  312.2 16.2 %all_to_all.83 = f32[32,1,289]{2,1,0:T(1,128)S(1)} all-to-all(f32[32,1,289]{2,1,0:T(1,128)S(1)} %broadcast_in_dim.255), channel_id=1, replica_groups=mesh['sub'=32,'crs'=8] {'sub'}, dimensions={0} | all-to-all | bytes 73984 | tf_op jit(solution)/shard_map/all_to_all | solution.py:30
  330.1 13.2 %all_to_all.84 = f32[8,1,73]{2,1,0:T(1,128)S(1)} all-to-all(f32[8,1,73]{2,1,0:T(1,128)S(1)} %broadcast_in_dim.256), channel_id=1, replica_groups=mesh['sub'=32,'crs'=8] {'crs'}, dimensions={0} | all-to-all | bytes 4672 | tf_op jit(solution)/shard_map/all_to_all | solution.py:30
  344.9 2.4 collective-permute-start.24
  347.3 1.3 collective-permute-start.25
  348.6 3.4 collective-permute-done.25
  (219 shorter events, 47.3 us)
Async XLA Ops:
  0.6 38.4 %copy-start = (f32[12,6,1536]{2,1,0:T(8,128)S(1)}, f32[12,6,1536]{2,1,0:T(8,128)}, u32[]{:S(2)}) copy-start(f32[12,6,1536]{2,1,0:T(8,128)} %param.9) | copy-start | bytes 1327108
  3.4 20.8 %all-to-all-start = ((f32[32,1,289]{2,1,0:T(1,128)}), f32[32,1,289]{2,1,0:T(1,128)S(1)}, u32[]{:S(2)}, u32[]{:S(2)}) async-start(f32[32,1,289]{2,1,0:T(1,128)} %broadcast_in_dim.238), calls=%async_computation | async-start | bytes 98304 | tf_op jit(solution)/shard_map/all_to_all | solution.py:30
  27.3 10.9 %all-to-all-start.1 = ((f32[8,1,73]{2,1,0:T(1,128)}), f32[8,1,73]{2,1,0:T(1,128)S(1)}, u32[]{:S(2)}, u32[]{:S(2)}) async-start(f32[8,1,73]{2,1,0:T(1,128)} %broadcast_in_dim.239), calls=%async_computation.1 | async-start | bytes 8192 | tf_op jit(solution)/shard_map/all_to_all | solution.py:30
  40.5 3.8 %collective-permute-start = (f32[1,72,128]{2,1,0:T(8,128)S(1)}, f32[1,72,128]{2,1,0:T(8,128)S(1)}, u32[]{:S(2)}, u32[]{:S(2)}) collective-permute-start(f32[1,72,128]{2,1,0:T(8,128)S(1)} %get-tuple-element.32), channel_id=1, source_target_pairs={{0,8},{8,16},{16,24},{24,32},{32,40},{40,48},{48,56},{56,64},{64,7... | collective-permute-start | bytes 110600 | tf_op jit(solution)/shard_map/ppermute | solution.py:14
  42.9 4.7 %collective-permute-start.1 = (f32[1,72,128]{2,1,0:T(8,128)S(1)}, f32[1,72,128]{2,1,0:T(8,128)S(1)}, u32[]{:S(2)}, u32[]{:S(2)}) collective-permute-start(f32[1,72,128]{2,1,0:T(8,128)S(1)} %get-tuple-element.33), channel_id=1, source_target_pairs={{8,0},{16,8},{24,16},{32,24},{40,32},{48,40},{56,48},{64,56},{72,6... | collective-permute-start | bytes 110600 | tf_op jit(solution)/shard_map/ppermute | solution.py:17
  47.6 34.0 %copy-start.2 = (f32[12,1536]{1,0:T(8,128)S(1)}, f32[12,1536]{1,0:T(8,128)}, u32[]{:S(2)}) copy-start(f32[12,1536]{1,0:T(8,128)} %param.14) | copy-start | bytes 221188
  49.2 3.8 %collective-permute-start.2 = (f32[1,72,128]{2,1,0:T(8,128)S(1)}, f32[1,72,128]{2,1,0:T(8,128)S(1)}, u32[]{:S(2)}, u32[]{:S(2)}) collective-permute-start(f32[1,72,128]{2,1,0:T(8,128)S(1)} %get-tuple-element.30), channel_id=1, source_target_pairs={{0,8},{8,16},{16,24},{24,32},{32,40},{40,48},{48,56},{56,64},{64,7... | collective-permute-start | bytes 110600 | tf_op jit(solution)/shard_map/ppermute | solution.py:14
  51.5 4.7 %collective-permute-start.3 = (f32[1,72,128]{2,1,0:T(8,128)S(1)}, f32[1,72,128]{2,1,0:T(8,128)S(1)}, u32[]{:S(2)}, u32[]{:S(2)}) collective-permute-start(f32[1,72,128]{2,1,0:T(8,128)S(1)} %get-tuple-element.31), channel_id=1, source_target_pairs={{8,0},{16,8},{24,16},{32,24},{40,32},{48,40},{56,48},{64,56},{72,6... | collective-permute-start | bytes 110600 | tf_op jit(solution)/shard_map/ppermute | solution.py:17
  56.9 36.3 %copy-start.3 = (s32[12]{0:T(128)S(1)}, s32[12]{0:T(128)}, u32[]{:S(2)}) copy-start(s32[12]{0:T(128)} %param.13) | copy-start | bytes 148
  56.9 36.5 %copy-start.1 = (f32[72,288]{1,0:T(8,128)S(1)}, f32[72,288]{1,0:T(8,128)}, u32[]{:S(2)}) copy-start(f32[72,288]{1,0:T(8,128)} %param.10) | copy-start | bytes 248836
  74.1 3.5 collective-permute-start.4
  76.2 4.8 %collective-permute-start.5 = (f32[1,72,128]{2,1,0:T(8,128)S(1)}, f32[1,72,128]{2,1,0:T(8,128)S(1)}, u32[]{:S(2)}, u32[]{:S(2)}) collective-permute-start(f32[1,72,128]{2,1,0:T(8,128)S(1)} %get-tuple-element.29), channel_id=1, source_target_pairs={{8,0},{16,8},{24,16},{32,24},{40,32},{48,40},{56,48},{64,56},{72,6... | collective-permute-start | bytes 110600 | tf_op jit(solution)/shard_map/ppermute | solution.py:17
  83.1 4.7 %collective-permute-start.6 = (f32[1,72,128]{2,1,0:T(8,128)S(1)}, f32[1,72,128]{2,1,0:T(8,128)S(1)}, u32[]{:S(2)}, u32[]{:S(2)}) collective-permute-start(f32[1,72,128]{2,1,0:T(8,128)S(1)} %get-tuple-element.26), channel_id=1, source_target_pairs={{0,8},{8,16},{16,24},{24,32},{32,40},{40,48},{48,56},{56,64},{64,7... | collective-permute-start | bytes 110600 | tf_op jit(solution)/shard_map/ppermute | solution.py:14
  86.5 4.7 %collective-permute-start.7 = (f32[1,72,128]{2,1,0:T(8,128)S(1)}, f32[1,72,128]{2,1,0:T(8,128)S(1)}, u32[]{:S(2)}, u32[]{:S(2)}) collective-permute-start(f32[1,72,128]{2,1,0:T(8,128)S(1)} %get-tuple-element.27), channel_id=1, source_target_pairs={{8,0},{16,8},{24,16},{32,24},{40,32},{48,40},{56,48},{64,56},{72,6... | collective-permute-start | bytes 110600 | tf_op jit(solution)/shard_map/ppermute | solution.py:17
  129.1 3.7 %collective-permute-start.8 = (f32[1,72,128]{2,1,0:T(8,128)S(1)}, f32[1,72,128]{2,1,0:T(8,128)S(1)}, u32[]{:S(2)}, u32[]{:S(2)}) collective-permute-start(f32[1,72,128]{2,1,0:T(8,128)S(1)} %get-tuple-element.24), channel_id=1, source_target_pairs={{0,8},{8,16},{16,24},{24,32},{32,40},{40,48},{48,56},{56,64},{64,7... | collective-permute-start | bytes 110600 | tf_op jit(solution)/shard_map/ppermute | solution.py:14
  131.6 4.7 %collective-permute-start.9 = (f32[1,72,128]{2,1,0:T(8,128)S(1)}, f32[1,72,128]{2,1,0:T(8,128)S(1)}, u32[]{:S(2)}, u32[]{:S(2)}) collective-permute-start(f32[1,72,128]{2,1,0:T(8,128)S(1)} %get-tuple-element.25), channel_id=1, source_target_pairs={{8,0},{16,8},{24,16},{32,24},{40,32},{48,40},{56,48},{64,56},{72,6... | collective-permute-start | bytes 110600 | tf_op jit(solution)/shard_map/ppermute | solution.py:17
  137.8 3.6 %collective-permute-start.10 = (f32[1,72,128]{2,1,0:T(8,128)S(1)}, f32[1,72,128]{2,1,0:T(8,128)S(1)}, u32[]{:S(2)}, u32[]{:S(2)}) collective-permute-start(f32[1,72,128]{2,1,0:T(8,128)S(1)} %get-tuple-element.22), channel_id=1, source_target_pairs={{0,8},{8,16},{16,24},{24,32},{32,40},{40,48},{48,56},{56,64},{64,7... | collective-permute-start | bytes 110600 | tf_op jit(solution)/shard_map/ppermute | solution.py:14
  140.1 4.7 %collective-permute-start.11 = (f32[1,72,128]{2,1,0:T(8,128)S(1)}, f32[1,72,128]{2,1,0:T(8,128)S(1)}, u32[]{:S(2)}, u32[]{:S(2)}) collective-permute-start(f32[1,72,128]{2,1,0:T(8,128)S(1)} %get-tuple-element.23), channel_id=1, source_target_pairs={{8,0},{16,8},{24,16},{32,24},{40,32},{48,40},{56,48},{64,56},{72,6... | collective-permute-start | bytes 110600 | tf_op jit(solution)/shard_map/ppermute | solution.py:17
  162.6 3.5 collective-permute-start.12
  164.7 4.8 %collective-permute-start.13 = (f32[1,72,128]{2,1,0:T(8,128)S(1)}, f32[1,72,128]{2,1,0:T(8,128)S(1)}, u32[]{:S(2)}, u32[]{:S(2)}) collective-permute-start(f32[1,72,128]{2,1,0:T(8,128)S(1)} %get-tuple-element.21), channel_id=1, source_target_pairs={{8,0},{16,8},{24,16},{32,24},{40,32},{48,40},{56,48},{64,56},{72,6... | collective-permute-start | bytes 110600 | tf_op jit(solution)/shard_map/ppermute | solution.py:17
  172.1 19.3 %all-to-all-start.6 = ((f32[32,1,1]{2,1,0:T(1,128)}), f32[32,1,1]{2,1,0:T(1,128)S(1)}, u32[]{:S(2)}, u32[]{:S(2)}) async-start(f32[32,1,1]{2,1,0:T(1,128)} %broadcast_in_dim.250), calls=%async_computation.6 | async-start | bytes 32768 | tf_op jit(solution)/shard_map/all_to_all | solution.py:30
  194.2 3.6 %collective-permute-start.14 = (f32[1,72,128]{2,1,0:T(8,128)S(1)}, f32[1,72,128]{2,1,0:T(8,128)S(1)}, u32[]{:S(2)}, u32[]{:S(2)}) collective-permute-start(f32[1,72,128]{2,1,0:T(8,128)S(1)} %get-tuple-element.18), channel_id=1, source_target_pairs={{0,8},{8,16},{16,24},{24,32},{32,40},{40,48},{48,56},{56,64},{64,7... | collective-permute-start | bytes 110600 | tf_op jit(solution)/shard_map/ppermute | solution.py:14
  196.4 4.7 %collective-permute-start.15 = (f32[1,72,128]{2,1,0:T(8,128)S(1)}, f32[1,72,128]{2,1,0:T(8,128)S(1)}, u32[]{:S(2)}, u32[]{:S(2)}) collective-permute-start(f32[1,72,128]{2,1,0:T(8,128)S(1)} %get-tuple-element.19), channel_id=1, source_target_pairs={{8,0},{16,8},{24,16},{32,24},{40,32},{48,40},{56,48},{64,56},{72,6... | collective-permute-start | bytes 110600 | tf_op jit(solution)/shard_map/ppermute | solution.py:17
  237.0 6.3 %collective-permute-start.16 = (f32[1,72,128]{2,1,0:T(8,128)S(1)}, f32[1,72,128]{2,1,0:T(8,128)S(1)}, u32[]{:S(2)}, u32[]{:S(2)}) collective-permute-start(f32[1,72,128]{2,1,0:T(8,128)S(1)} %get-tuple-element.16), channel_id=1, source_target_pairs={{0,8},{8,16},{16,24},{24,32},{32,40},{40,48},{48,56},{56,64},{64,7... | collective-permute-start | bytes 110600 | tf_op jit(solution)/shard_map/ppermute | solution.py:14
  239.4 4.7 %collective-permute-start.17 = (f32[1,72,128]{2,1,0:T(8,128)S(1)}, f32[1,72,128]{2,1,0:T(8,128)S(1)}, u32[]{:S(2)}, u32[]{:S(2)}) collective-permute-start(f32[1,72,128]{2,1,0:T(8,128)S(1)} %get-tuple-element.17), channel_id=1, source_target_pairs={{8,0},{16,8},{24,16},{32,24},{40,32},{48,40},{56,48},{64,56},{72,6... | collective-permute-start | bytes 110600 | tf_op jit(solution)/shard_map/ppermute | solution.py:17
  245.7 4.5 %collective-permute-start.18 = (f32[1,72,128]{2,1,0:T(8,128)S(1)}, f32[1,72,128]{2,1,0:T(8,128)S(1)}, u32[]{:S(2)}, u32[]{:S(2)}) collective-permute-start(f32[1,72,128]{2,1,0:T(8,128)S(1)} %get-tuple-element.14), channel_id=1, source_target_pairs={{0,8},{8,16},{16,24},{24,32},{32,40},{40,48},{48,56},{56,64},{64,7... | collective-permute-start | bytes 110600 | tf_op jit(solution)/shard_map/ppermute | solution.py:14
  248.9 4.7 %collective-permute-start.19 = (f32[1,72,128]{2,1,0:T(8,128)S(1)}, f32[1,72,128]{2,1,0:T(8,128)S(1)}, u32[]{:S(2)}, u32[]{:S(2)}) collective-permute-start(f32[1,72,128]{2,1,0:T(8,128)S(1)} %get-tuple-element.15), channel_id=1, source_target_pairs={{8,0},{16,8},{24,16},{32,24},{40,32},{48,40},{56,48},{64,56},{72,6... | collective-permute-start | bytes 110600 | tf_op jit(solution)/shard_map/ppermute | solution.py:17
  270.6 3.7 %collective-permute-start.20 = (f32[1,72,128]{2,1,0:T(8,128)S(1)}, f32[1,72,128]{2,1,0:T(8,128)S(1)}, u32[]{:S(2)}, u32[]{:S(2)}) collective-permute-start(f32[1,72,128]{2,1,0:T(8,128)S(1)} %get-tuple-element.12), channel_id=1, source_target_pairs={{0,8},{8,16},{16,24},{24,32},{32,40},{40,48},{48,56},{56,64},{64,7... | collective-permute-start | bytes 110600 | tf_op jit(solution)/shard_map/ppermute | solution.py:14
  272.8 4.7 %collective-permute-start.21 = (f32[1,72,128]{2,1,0:T(8,128)S(1)}, f32[1,72,128]{2,1,0:T(8,128)S(1)}, u32[]{:S(2)}, u32[]{:S(2)}) collective-permute-start(f32[1,72,128]{2,1,0:T(8,128)S(1)} %get-tuple-element.13), channel_id=1, source_target_pairs={{8,0},{16,8},{24,16},{32,24},{40,32},{48,40},{56,48},{64,56},{72,6... | collective-permute-start | bytes 110600 | tf_op jit(solution)/shard_map/ppermute | solution.py:17
  302.1 3.6 %collective-permute-start.22 = (f32[1,72,128]{2,1,0:T(8,128)S(1)}, f32[1,72,128]{2,1,0:T(8,128)S(1)}, u32[]{:S(2)}, u32[]{:S(2)}) collective-permute-start(f32[1,72,128]{2,1,0:T(8,128)S(1)} %get-tuple-element.10), channel_id=1, source_target_pairs={{0,8},{8,16},{16,24},{24,32},{32,40},{40,48},{48,56},{56,64},{64,7... | collective-permute-start | bytes 110600 | tf_op jit(solution)/shard_map/ppermute | solution.py:14
  304.3 4.7 %collective-permute-start.23 = (f32[1,72,128]{2,1,0:T(8,128)S(1)}, f32[1,72,128]{2,1,0:T(8,128)S(1)}, u32[]{:S(2)}, u32[]{:S(2)}) collective-permute-start(f32[1,72,128]{2,1,0:T(8,128)S(1)} %get-tuple-element.11), channel_id=1, source_target_pairs={{8,0},{16,8},{24,16},{32,24},{40,32},{48,40},{56,48},{64,56},{72,6... | collective-permute-start | bytes 110600 | tf_op jit(solution)/shard_map/ppermute | solution.py:17
  344.9 3.7 %collective-permute-start.24 = (f32[1,72,128]{2,1,0:T(8,128)S(1)}, f32[1,72,128]{2,1,0:T(8,128)S(1)}, u32[]{:S(2)}, u32[]{:S(2)}) collective-permute-start(f32[1,72,128]{2,1,0:T(8,128)S(1)} %get-tuple-element.8), channel_id=1, source_target_pairs={{0,8},{8,16},{16,24},{24,32},{32,40},{40,48},{48,56},{56,64},{64,7... | collective-permute-start | bytes 110600 | tf_op jit(solution)/shard_map/ppermute | solution.py:14
  347.3 4.7 %collective-permute-start.25 = (f32[1,72,128]{2,1,0:T(8,128)S(1)}, f32[1,72,128]{2,1,0:T(8,128)S(1)}, u32[]{:S(2)}, u32[]{:S(2)}) collective-permute-start(f32[1,72,128]{2,1,0:T(8,128)S(1)} %get-tuple-element.9), channel_id=1, source_target_pairs={{8,0},{16,8},{24,16},{32,24},{40,32},{48,40},{56,48},{64,56},{72,6... | collective-permute-start | bytes 110600 | tf_op jit(solution)/shard_map/ppermute | solution.py:17
where the time goes:
time: 356 us; the launch traced here: 353 us
  blocking collectives  143 us (40%)
  starting transfers between devices  77.8 us (22%)
  waiting for transfers between devices  57.5 us (16%)
  local copies, waits for them, and re-layouts  25.4 us (7%)
  matrix products  24.6 us (7%)
  other arithmetic  19.5 us (5%)
  between operations  5.8 us (2%)
    all_to_all x10, blocking collectives, copy_for_each(): lax.all_to_all(jnp.broadcast_to(shard[None], (count, *shard.shape)), axis...  143 us
    ppermute x13, waiting for transfers between devices, with_halo(): lax.ppermute(lax.slice_in_dim(block, 0, width, axis=dim), axis, backward)  41.1 us
    ppermute x13, starting transfers between devices, with_halo(): lax.ppermute(lax.slice_in_dim(block, block.shape[dim] - width, None, axis...  31.9 us
    all_to_all x3, starting transfers between devices, copy_for_each(): lax.all_to_all(jnp.broadcast_to(shard[None], (count, *shard.shape)), axis...  29.1 us
    ppermute x13, starting transfers between devices, with_halo(): lax.ppermute(lax.slice_in_dim(block, 0, width, axis=dim), axis, backward)  16.8 us
    all_to_all x3, waiting for transfers between devices, copy_for_each(): lax.all_to_all(jnp.broadcast_to(shard[None], (count, *shard.shape)), axis...  16.4 us
    dot_general x3, matrix products, operator(): jnp.einsum('srk,sk->sr', dual_ops, lowered, preferred_element_type=jnp.fl...  14.8 us
    gather x26, local copies, waits for them, and re-layouts, jump(): gathered[source]  8.8 us
  transfers between devices with their start and end apart: 29, of which 16 were waited for; matrix products, arithmetic and copies ran while one was open for 2% of the time, Pallas kernels for 0%

commit v1 on v0

v1 whole, which is shorter than its diff:
```python
import functools

import jax
import jax.numpy as jnp
from jax import lax
from jax.experimental import pallas as pl
from jax.experimental.pallas import tpu as pltpu
from jax.sharding import PartitionSpec as P

ITERATIONS = 2
LANES = 128
F32 = jnp.float32


def lane_sum(a):
    return jnp.sum(a, axis=1, keepdims=True)


def total(a):
    return jnp.sum(lane_sum(a), axis=0, keepdims=True)


def kernel(
    n_sub, n_crs,
    partner, sends, modes, load, ops_hbm, traces, factor, rhs,
    out_m, out_p,
    ops, tk, wk, gather, mate, res, jres, way, jway,
    cmsg, crecv, xmsg, xrecv, qmsg, qrecv, hmsg, hrecv,
    ops_sem, c_send, c_recv, x_send, x_recv, q_send, q_recv, h_send, h_recv,
):
    n_s, n_row, order = ops.shape
    n_b = order // LANES
    n_local = n_s * n_b
    n_k = tk.shape[0]
    n_col = factor.shape[1]
    slots = sends.shape[1]
    sub = lax.axis_index("sub")
    crs = lax.axis_index("crs")

    fetch = pltpu.make_async_copy(ops_hbm, ops, ops_sem)
    fetch.start()

    barrier = pltpu.get_barrier_semaphore()

    def greet(axis, me, count):
        def one(t, carry):
            pl.semaphore_signal(
                barrier, inc=1, device_id={axis: lax.rem(me + t, count)},
                device_id_type=pl.DeviceIdType.MESH,
            )
            return carry
        lax.fori_loop(1, count, one, 0)

    greet("sub", sub, n_sub)
    greet("crs", crs, n_crs)

    def copy(src, dst, send, recv, where):
        return pltpu.make_async_remote_copy(
            src_ref=src, dst_ref=dst, send_sem=send, recv_sem=recv,
            device_id=where, device_id_type=pl.DeviceIdType.MESH,
        )

    def spread(msg, slots_ref, send, recv, axis, me, count):
        def one(t, carry):
            copy(msg, slots_ref.at[t - 1], send, recv, {axis: lax.rem(me + t, count)}).start()
            return carry
        lax.fori_loop(1, count, one, 0)

    def arrivals(slots_ref, send, recv, axis, me, count):
        whole = slots_ref.at[pl.ds(0, count - 1)]
        return copy(whole, whole, send, recv, {axis: lax.rem(me + 1, count)})

    def slot_of(who, me, count):
        return lax.rem(me - who - 1 + count, count)

    def jump_start(v, j):
        for b in range(n_b):
            gather[pl.ds(b, n_s, stride=n_b), :] = v[:, b * LANES:(b + 1) * LANES]

        def pick(n, carry):
            for side in range(2):
                for m in range(8):
                    at = jnp.maximum(sends[side, n * 8 + m], 0)
                    hmsg[j, side, pl.ds(n * 8 + m, 1), :] = gather[pl.ds(at, 1), :]
            return carry
        lax.fori_loop(0, slots // 8, pick, 0)
        for side in range(2):
            there = lax.rem(sub + (n_sub - 1 if side == 0 else 1), n_sub)
            copy(hmsg.at[j, side], hrecv.at[j, 1 - side], h_send.at[j, side], h_recv.at[j, 1 - side],
                 {"sub": there}).start()

    def jump_end(v, j):
        for side in range(2):
            there = lax.rem(sub + 1, n_sub)
            copy(hmsg.at[j, side], hrecv.at[j, side], h_send.at[j, side], h_recv.at[j, side],
                 {"sub": there}).wait_recv()
            gather[pl.ds(n_local + side * slots, slots), :] = hrecv[j, side]

        def pair(s, carry):
            for b in range(n_b):
                code = partner[s, b]
                at = jnp.where(code < 0, s * n_b + b, code)
                mate[pl.ds(s * n_b + b, 1), :] = gather[pl.ds(at, 1), :]
            return carry
        lax.fori_loop(0, n_s, pair, 0)
        parts = [mate[pl.ds(b, n_s, stride=n_b), :] for b in range(n_b)]
        return v - jnp.concatenate(parts, axis=1)

    def pad_col(col):
        parts = []
        for n in range(3):
            piece = col[:, n * LANES:min((n + 1) * LANES, n_col)]
            if piece.shape[1] < LANES:
                piece = jnp.concatenate([piece, jnp.zeros((1, LANES - piece.shape[1]), F32)], axis=1)
            parts.append(piece)
        return parts

    lane = lax.broadcasted_iota(jnp.int32, (1, LANES), 1)

    def sub_start(n, col, scalars):
        for at, piece in enumerate(pad_col(col)):
            cmsg[n, at:at + 1, :] = piece
        last = jnp.zeros((1, LANES), F32)
        for at, value in enumerate(scalars):
            last = jnp.where(lane == at, value, last)
        cmsg[n, 3:4, :] = last
        crecv[n, n_sub - 1] = cmsg[n]
        spread(cmsg.at[n], crecv.at[n], c_send.at[n], c_recv.at[n], "sub", sub, n_sub)

    def sub_end(n):
        arrivals(crecv.at[n], c_send.at[n], c_recv.at[n], "sub", sub, n_sub).wait_recv()
        got = [crecv[n, slot_of(who, sub, n_sub)] for who in range(n_sub)]
        while len(got) > 1:
            got = [got[i] + got[i + 1] for i in range(0, len(got), 2)]
        tot = got[0]
        col = jnp.concatenate([tot[0:1], tot[1:2], tot[2:3, :n_col - 2 * LANES]], axis=1)
        return col, tot[3:4]

    wide = lax.broadcasted_iota(jnp.int32, (n_s, LANES), 1)
    tall = lax.broadcasted_iota(jnp.int32, (n_s, LANES), 0)

    def back(n, col):
        mix = jnp.zeros((n_s, LANES), F32)
        for k in range(n_k):
            mix = jnp.where(wide == k, lane_sum(wk[k] * col), mix)
        folded = lane_sum(col * col)
        mix = jnp.where((wide == n_k) & (tall == 0), folded, mix)
        xmsg[n] = mix
        xrecv[n, n_crs - 1] = mix
        spread(xmsg.at[n], xrecv.at[n], x_send.at[n], x_recv.at[n], "crs", crs, n_crs)

    def back_end(n):
        arrivals(xrecv.at[n], x_send.at[n], x_recv.at[n], "crs", crs, n_crs).wait_recv()
        tot = xrecv[n, slot_of(0, crs, n_crs)]
        for who in range(1, n_crs):
            tot = tot + xrecv[n, slot_of(who, crs, n_crs)]
        return tot

    def expand(tot, j):
        z = tk[0] * tot[:, 0:1]
        for k in range(1, n_k):
            z = z + tk[k] * tot[:, k:k + 1]
        jump_start(z, j)
        return jump_end(z, j)

    def restrict_col(jv):
        acc = None
        for k in range(n_k):
            e = lane_sum(tk[k] * jv)
            term = wk[k] * e
            acc = term if acc is None else acc + term
        return jnp.sum(acc, axis=0, keepdims=True)

    odd = lax.rem(crs, 2) == 1

    def operator(ju, n, j):
        row = lax.broadcasted_iota(jnp.int32, ju.shape, 0)
        acc = jnp.zeros((n_s, n_row), F32)
        for s in range(n_s):
            u = jnp.where(row == s, ju, 0.0).astype(jnp.bfloat16)
            acc = acc + lax.dot_general(u, ops[s], (((1,), (1,)), ((), ())), preferred_element_type=F32)
        blank = jnp.zeros((n_s, 2 * LANES - n_row), F32)
        lined = jnp.where(odd, jnp.concatenate([blank, acc], axis=1), jnp.concatenate([acc, blank], axis=1))
        for half in range(2):
            piece = lined[:, half * LANES:(half + 1) * LANES]
            qmsg[n, half] = piece
            qrecv[n, n_crs - 1, half] = piece
        spread(qmsg.at[n], qrecv.at[n], q_send.at[n], q_recv.at[n], "crs", crs, n_crs)
        arrivals(qrecv.at[n], q_send.at[n], q_recv.at[n], "crs", crs, n_crs).wait_recv()
        blocks = []
        for pair in range(n_crs // 2):
            even, uneven = slot_of(2 * pair, crs, n_crs), slot_of(2 * pair + 1, crs, n_crs)
            blocks.append(qrecv[n, even, 0])
            blocks.append(jnp.where(wide < LANES // 2, qrecv[n, even, 1], qrecv[n, uneven, 0]))
            blocks.append(qrecv[n, uneven, 1])
        q = jnp.concatenate(blocks, axis=1)
        jump_start(q, j)
        return jump_end(q, j)

    for s in range(n_s):
        for k in range(n_k):
            keep = jnp.where(k < modes[s], 1.0, 0.0).astype(F32)
            tk[k, s:s + 1, :] = traces[s, k:k + 1, :] * keep
            wk[k, s:s + 1, :] = factor[s * n_k + k:s * n_k + k + 1, :]
    col = jnp.zeros((1, n_col), F32)
    for s in range(n_s):
        for k in range(n_k):
            keep = jnp.where(k < modes[s], load[s * n_k + k], 0.0)
            col = col + factor[s * n_k + k:s * n_k + k + 1, :] * keep

    pl.semaphore_wait(barrier, n_sub - 1 + n_crs - 1)

    sub_start(0, col, ())
    jump_start(rhs, 0)
    jrhs = jump_end(rhs[...], 0)
    jres[...] = jrhs
    col, _ = sub_end(0)
    back(0, col)
    fetch.wait()
    mult = expand(back_end(0), 1)
    out_m[...] = mult
    applied = operator(2.0 * mult, 0, 2)
    r = rhs[...] - applied
    jr = jres[...] - 2.0 * applied
    res[...] = r
    jres[...] = jr
    sub_start(1, restrict_col(jr), (total(r * r),))
    col, tail = sub_end(1)
    square = tail[:, 0:1]
    back(1, col)
    tot = back_end(1)
    rw = square - tot[0:1, n_k:n_k + 1]
    lifted = expand(tot, 3)
    way[...] = res[...] - lifted
    jway[...] = jres[...] - 2.0 * lifted
    for turn in range(ITERATIONS):
        applied = operator(jway[...], 1 + turn, 4 + 2 * turn)
        d, r = way[...], res[...]
        sub_start(2 + turn, restrict_col(2.0 * applied),
                  (total(d * applied), total(r * applied), total(applied * applied)))
        change, tail = sub_end(2 + turn)
        alpha = rw / tail[:, 0:1]
        col = col - alpha * change
        back(2 + turn, col)
        square = square - 2.0 * alpha * tail[:, 1:2] + alpha * alpha * tail[:, 2:3]
        r = res[...] - alpha * applied
        jr = jres[...] - 2.0 * alpha * applied
        res[...] = r
        jres[...] = jr
        out_m[...] = out_m[...] + alpha * way[...]
        tot = back_end(2 + turn)
        lifted = expand(tot, 5 + 2 * turn)
        if turn == ITERATIONS - 1:
            out_p[...] = res[...] - lifted
        else:
            following = square - tot[0:1, n_k:n_k + 1]
            beta = following / rw
            way[...] = res[...] - lifted + beta * way[...]
            jway[...] = jres[...] - 2.0 * lifted + beta * jway[...]
            rw = following

    for n in range(ITERATIONS + 2):
        arrivals(crecv.at[n], c_send.at[n], c_recv.at[n], "sub", sub, n_sub).wait_send()
        arrivals(xrecv.at[n], x_send.at[n], x_recv.at[n], "crs", crs, n_crs).wait_send()
    for n in range(ITERATIONS + 1):
        arrivals(qrecv.at[n], q_send.at[n], q_recv.at[n], "crs", crs, n_crs).wait_send()
    for j in range(2 * ITERATIONS + 4):
        for side in range(2):
            copy(hmsg.at[j, side], hrecv.at[j, side], h_send.at[j, side], h_recv.at[j, side],
                 {"sub": lax.rem(sub + 1, n_sub)}).wait_send()


def local(n_sub, n_crs, ops, traces, factor, partner, sends, modes, rhs, load):
    n_s, n_row, order = ops.shape
    n_k = traces.shape[1]
    n_col = factor.shape[1]
    slots = sends.shape[1]
    n_local = n_s * order // LANES
    n_c, n_q, n_j = ITERATIONS + 2, ITERATIONS + 1, 2 * ITERATIONS + 4
    smem = pl.BlockSpec(memory_space=pltpu.SMEM)
    vmem = pl.BlockSpec(memory_space=pltpu.VMEM)
    dma = pltpu.SemaphoreType.DMA
    vector = (n_s, order)
    return pl.pallas_call(
        functools.partial(kernel, n_sub, n_crs),
        out_shape=(jax.ShapeDtypeStruct(vector, F32), jax.ShapeDtypeStruct(vector, F32)),
        in_specs=[smem, smem, smem, smem, pl.BlockSpec(memory_space=pl.ANY), vmem, vmem, vmem],
        out_specs=(vmem, vmem),
        scratch_shapes=[
            pltpu.VMEM(ops.shape, ops.dtype),
            pltpu.VMEM((n_k, n_s, order), F32),
            pltpu.VMEM((n_k, n_s, n_col), F32),
            pltpu.VMEM((n_local + 2 * slots, LANES), F32),
            pltpu.VMEM((n_local, LANES), F32),
            pltpu.VMEM(vector, F32),
            pltpu.VMEM(vector, F32),
            pltpu.VMEM(vector, F32),
            pltpu.VMEM(vector, F32),
            pltpu.VMEM((n_c, 4, LANES), F32),
            pltpu.VMEM((n_c, n_sub, 4, LANES), F32),
            pltpu.VMEM((n_c, n_s, LANES), F32),
            pltpu.VMEM((n_c, n_crs, n_s, LANES), F32),
            pltpu.VMEM((n_q, 2, n_s, LANES), F32),
            pltpu.VMEM((n_q, n_crs, 2, n_s, LANES), F32),
            pltpu.VMEM((n_j, 2, slots, LANES), F32),
            pltpu.VMEM((n_j, 2, slots, LANES), F32),
            dma, dma((n_c,)), dma((n_c,)), dma((n_c,)), dma((n_c,)), dma((n_q,)), dma((n_q,)),
            dma((n_j, 2)), dma((n_j, 2)),
        ],
        compiler_params=pltpu.CompilerParams(
            collective_id=0, has_side_effects=True, vmem_limit_bytes=48 * 1024 * 1024
        ),
    )(partner, sends, modes, load, ops, traces, factor, rhs)


def solution(mesh):
    return jax.shard_map(
        functools.partial(local, mesh.shape["sub"], mesh.shape["crs"]),
        mesh=mesh,
        in_specs=(
            P("sub", "crs", None),
            P("sub", None, None),
            P("sub", "crs"),
            P("sub", None),
            P("sub", None),
            P("sub"),
            P("sub", None),
            P("sub"),
        ),
        out_specs=(P("sub", None), P("sub", None)),
        check_vma=False,
    )
```

time: 356 us -> 113 us (0.32)
  blocking collectives: 143 us -> 0 us
  Pallas kernels: 0 us -> 105 us
  starting transfers between devices: 77.8 us -> 0 us
  waiting for transfers between devices: 57.5 us -> 0 us
  matrix products: 24.6 us -> 0 us
  other arithmetic: 19.5 us -> 0 us
  local copies, waits for them, and re-layouts: 25.4 us -> 6.81 us
  between operations: 5.8 us -> 0.66 us
    all_to_all x10 -> x0, blocking collectives: 143 us -> none  [copy_for_each(): lax.all_to_all(jnp.broadcast_to(shard[None], (count, *shard.shape)), axis...]
    pallas_call x0 -> x1, Pallas kernels: none -> 105 us  [local(): pl.pallas_call(functools.partial(kernel, n_sub, n_crs), out_shape=(jax.Sh...]
    ppermute x26 -> x0, starting transfers between devices: 48.7 us -> none  [the longest x13 31.9 us: with_halo(): lax.ppermute(lax.slice_in_dim(block, block.shape[dim] - width, None, axis...]
    ppermute x26 -> x0, waiting for transfers between devices: 41.1 us -> none  [the longest x13 41.1 us: with_halo(): lax.ppermute(lax.slice_in_dim(block, 0, width, axis=dim), axis, backward)]
    all_to_all x3 -> x0, starting transfers between devices: 29.1 us -> none  [copy_for_each(): lax.all_to_all(jnp.broadcast_to(shard[None], (count, *shard.shape)), axis...]
    dot_general x18 -> x0, matrix products: 24.6 us -> none  [the longest x3 14.8 us: operator(): jnp.einsum('srk,sk->sr', dual_ops, lowered, preferred_element_type=jnp.fl...]
    gather x39 -> x0, local copies, waits for them, and re-layouts: 17.4 us -> none  [the longest x26 8.8 us: jump(): gathered[source]]
    all_to_all x3 -> x0, waiting for transfers between devices: 16.4 us -> none  [copy_for_each(): lax.all_to_all(jnp.broadcast_to(shard[None], (count, *shard.shape)), axis...]
  transfers between devices with their start and end apart: 29 -> 0, of which waited for: 16 -> 0; matrix products, arithmetic and copies ran while one was open for 2% -> 0% of each run, Pallas kernels for 0% -> 0%
where the time goes in v1:
time: 113 us
  Pallas kernels  105 us (93%)
  local copies, waits for them, and re-layouts  6.81 us (6%)
    pallas_call x1, Pallas kernels, local(): pl.pallas_call(functools.partial(kernel, n_sub, n_crs), out_shape=(jax.Sh...  105 us
    unnamed x16, local copies, waits for them, and re-layouts  6.81 us

profile of v1, /device:TPU:1, one launch (start us, length us, event | category | flops | bytes accessed | tf_op | source)
XLA Modules:
  0.0 112.9 jit_solution(382926905260865808)
XLA Ops:
  0.6 0.0 copy-start
  0.6 1.1 copy-done
  1.7 0.0 copy-start.1
  1.7 0.9 copy-done.1
  2.6 0.0 copy-start.2
  2.6 0.9 copy-done.2
  3.5 0.0 copy-start.3
  3.5 0.7 copy-done.3
  4.2 0.0 copy-start.4
  4.2 0.7 copy-done.4
  4.9 0.0 copy-start.5
  4.9 0.7 copy-done.5
  5.5 0.0 copy-start.6
  5.5 0.7 copy-done.6
  6.2 105.4 %shard_map.95 = (f32[12,1536]{1,0:T(8,128)S(1)}, f32[12,1536]{1,0:T(8,128)S(1)}) custom-call(s32[12,12]{1,0:T(8,128)S(1)} %copy-done.3, s32[2,72]{1,0:T(2,128)S(1)} %copy-done.4, s32[12]{0:T(128)S(1)} %copy-done.5, f32[72]{0:T(128)S(1)} %copy-done.6, bf16[12,192,1536]{2,1,0:T(8,128)(2,1)} %ops_hbm.1, f32[12,6,1536]{2,1,0:T(8,128)S(1)} %copy-done, ...), custom_call_target="tpu_custom_call" | custom-call | tf_op jit(solution)/shard_map/pallas_call | solution.py:284
  111.6 0.6 copy.12
  112.2 0.6 copy.13
Async XLA Ops:
  0.6 1.1 copy-start
  1.7 0.9 copy-start.1
  2.6 0.9 copy-start.2
  3.5 0.7 copy-start.3
  4.2 0.7 copy-start.4
  4.9 0.7 copy-start.5
  5.5 0.7 copy-start.6

commit v2 on v1

v2 whole, which is shorter than its diff:
```python
import functools

import jax
import jax.numpy as jnp
from jax import lax
from jax.experimental import pallas as pl
from jax.experimental.pallas import tpu as pltpu
from jax.sharding import PartitionSpec as P

ITERATIONS = 2
LANES = 128
F32 = jnp.float32


def lane_sum(a):
    return jnp.sum(a, axis=1, keepdims=True)


def total(a):
    return jnp.sum(lane_sum(a), axis=0, keepdims=True)


def kernel(
    n_sub, n_crs,
    partner_in, sends_in, modes_in, load_in, ops_in, traces_in, factor_in, rhs_in,
    out_m, out_p,
    partner, sends, modes, load, ops, traces, factor, rhs,
    tk, tl, tp, wk, planes, mates, member, member_t, inner, gather, mate, lift, qv, res, jres, way, jway,
    cmsg, crecv, xmsg, xrecv, qmsg, qrecv, hmsg, hrecv, tmsg, trecv, wrecv, rmsg, rrecv,
    in_sem, c_send, c_recv, x_send, x_recv, q_send, q_recv, h_send, h_recv, t_send, t_recv, w_send, w_recv,
    r_send, r_recv,
):
    n_s, n_row, order = ops.shape
    n_b = order // LANES
    n_local = n_s * n_b
    n_k = tk.shape[0]
    n_col = factor.shape[1]
    slots = sends.shape[1]
    tile = 16
    sub = lax.axis_index("sub")
    crs = lax.axis_index("crs")

    pairs = ((partner_in, partner), (sends_in, sends), (modes_in, modes), (load_in, load),
             (factor_in, factor), (traces_in, traces), (rhs_in, rhs), (ops_in, ops))
    fetch = [pltpu.make_async_copy(a, b, in_sem.at[n]) for n, (a, b) in enumerate(pairs)]
    for one in fetch:
        one.start()

    barrier = pltpu.get_barrier_semaphore()

    def greet(axis, me, count):
        def one(t, carry):
            pl.semaphore_signal(
                barrier, inc=1, device_id={axis: lax.rem(me + t, count)},
                device_id_type=pl.DeviceIdType.MESH,
            )
            return carry
        lax.fori_loop(1, count, one, 0)

    greet("sub", sub, n_sub)
    greet("crs", crs, n_crs)

    def copy(src, dst, send, recv, where):
        return pltpu.make_async_remote_copy(
            src_ref=src, dst_ref=dst, send_sem=send, recv_sem=recv,
            device_id=where, device_id_type=pl.DeviceIdType.MESH,
        )

    def spread(msg, slots_ref, send, recv, axis, me, count):
        def one(t, carry):
            copy(msg, slots_ref.at[t - 1], send, recv, {axis: lax.rem(me + t, count)}).start()
            return carry
        lax.fori_loop(1, count, one, 0)

    def arrivals(slots_ref, send, recv, axis, me, count):
        whole = slots_ref.at[pl.ds(0, count - 1)]
        return copy(whole, whole, send, recv, {axis: lax.rem(me + 1, count)})

    def slot_of(who, me, count):
        return lax.rem(me - who - 1 + count, count)

    before, after = lax.rem(sub + n_sub - 1, n_sub), lax.rem(sub + 1, n_sub)

    def both(msg, recv_ref, send, recv):
        return [copy(msg[0], recv_ref.at[1], send.at[0], recv.at[1], {"sub": before}),
                copy(msg[1], recv_ref.at[0], send.at[1], recv.at[0], {"sub": after})]

    def rows_of(v, b):
        return v[:, b * LANES:(b + 1) * LANES]

    def jump_start(v, j):
        for b in range(n_b):
            gather[pl.ds(b, n_s, stride=n_b), :] = rows_of(v, b)

        def pick(n, carry):
            for side in range(2):
                for m in range(8):
                    at = jnp.maximum(sends[side, n * 8 + m], 0)
                    hmsg[j, side, pl.ds(n * 8 + m, 1), :] = gather[pl.ds(at, 1), :]
            return carry
        lax.fori_loop(0, slots // 8, pick, 0)

    def jump_copies(j):
        return both((hmsg.at[j, 0], hmsg.at[j, 1]), hrecv.at[j], h_send.at[j], h_recv.at[j])

    def jump_end(v, j):
        one, two = jump_copies(j)
        one.wait_recv()
        two.wait_recv()
        for side in range(2):
            gather[pl.ds(n_local + side * slots, slots), :] = hrecv[j, side]

        def pair(s, carry):
            for b in range(n_b):
                code = partner[s, b]
                at = jnp.where(code < 0, s * n_b + b, code)
                mate[pl.ds(s * n_b + b, 1), :] = gather[pl.ds(at, 1), :]
            return carry
        lax.fori_loop(0, n_s, pair, 0)
        parts = [mate[pl.ds(b, n_s, stride=n_b), :] for b in range(n_b)]
        return v - jnp.concatenate(parts, axis=1)

    lane = lax.broadcasted_iota(jnp.int32, (1, LANES), 1)
    wide = lax.broadcasted_iota(jnp.int32, (n_s, LANES), 1)

    def sub_start(n, col, scalars):
        for at in range(3):
            piece = col[:, at * LANES:min((at + 1) * LANES, n_col)]
            if piece.shape[1] < LANES:
                piece = jnp.concatenate([piece, jnp.zeros((1, LANES - piece.shape[1]), F32)], axis=1)
            cmsg[n, at:at + 1, :] = piece
        last = jnp.zeros((1, LANES), F32)
        for at, value in enumerate(scalars):
            last = jnp.where(lane == at, value, last)
        cmsg[n, 3:4, :] = last
        crecv[n, n_sub - 1] = cmsg[n]
        spread(cmsg.at[n], crecv.at[n], c_send.at[n], c_recv.at[n], "sub", sub, n_sub)

    def tree(got):
        while len(got) > 1:
            got = [got[i] + got[i + 1] for i in range(0, len(got), 2)]
        return got[0]

    def sub_end(n):
        arrivals(crecv.at[n], c_send.at[n], c_recv.at[n], "sub", sub, n_sub).wait_recv()
        tot = tree([crecv[n, slot_of(who, sub, n_sub)] for who in range(n_sub)])
        col = jnp.concatenate([tot[0:1], tot[1:2], tot[2:3, :n_col - 2 * LANES]], axis=1)
        return col, tot[3:4]

    def square_start(n, v):
        line = jnp.where(lane == 0, total(v * v), 0.0)
        rmsg[n] = line
        rrecv[n, n_sub - 1] = line
        spread(rmsg.at[n], rrecv.at[n], r_send.at[n], r_recv.at[n], "sub", sub, n_sub)

    def square_end(n):
        arrivals(rrecv.at[n], r_send.at[n], r_recv.at[n], "sub", sub, n_sub).wait_recv()
        return tree([rrecv[n, slot_of(who, sub, n_sub)] for who in range(n_sub)])[:, 0:1]

    n_x = 3 * n_k
    fold_at = 2 * n_x + 4

    def back(n, col):
        mix = jnp.zeros((n_s, LANES), F32)
        for near in range(3):
            for k in range(n_k):
                mix = jnp.where(wide == near * n_k + k, lane_sum(wk[near, k] * col), mix)
        low = jnp.concatenate([mix[8:n_s], jnp.zeros((16 - n_s, LANES), F32)], axis=0)
        msg = mix[0:8] + pltpu.roll(low, n_x, 1)
        at = (lax.broadcasted_iota(jnp.int32, (8, LANES), 1) == fold_at) & (
            lax.broadcasted_iota(jnp.int32, (8, LANES), 0) == 0)
        msg = jnp.where(at, lane_sum(col * col), msg)
        xmsg[n] = msg
        xrecv[n, n_crs - 1] = msg
        spread(xmsg.at[n], xrecv.at[n], x_send.at[n], x_recv.at[n], "crs", crs, n_crs)

    def back_end(n):
        arrivals(xrecv.at[n], x_send.at[n], x_recv.at[n], "crs", crs, n_crs).wait_recv()
        tot = tree([xrecv[n, slot_of(who, crs, n_crs)] for who in range(n_crs)])
        low = pltpu.roll(tot, LANES - n_x, 1)
        return jnp.concatenate([tot, low[:n_s - 8]], axis=0), tot[0:1, fold_at:fold_at + 1]

    def expand(mix):
        spare = jnp.zeros((tile - n_s, LANES), F32)
        rows = []
        for near in range(3):
            rows += [pltpu.roll(mix, LANES - near * n_k, 1) if near else mix, spare]
        rows.append(jnp.zeros((LANES - 3 * tile, LANES), F32))
        mates_x = jnp.dot(member[...], jnp.concatenate(rows, axis=0), precision=lax.Precision.HIGHEST,
                          preferred_element_type=F32)
        own = [mix[:, n_k + k:n_k + k + 1] for k in range(n_k)]
        for b in range(n_b):
            theirs = mates_x[b * tile:b * tile + n_s]
            acc = None
            for k in range(n_k):
                term = rows_of(tl[k], b) * own[k] - rows_of(tp[k], b) * theirs[:, k:k + 1]
                acc = term if acc is None else acc + term
            lift[:, b * LANES:(b + 1) * LANES] = acc

    def restrict_col(jv):
        acc = None
        for k in range(n_k):
            term = wk[1, k] * lane_sum(tl[k] * jv)
            acc = term if acc is None else acc + term
        return jnp.sum(acc, axis=0, keepdims=True)

    def adjoint_col(q):
        for b in range(n_b):
            line = jnp.zeros((n_s, LANES), F32)
            for k in range(n_k):
                line = jnp.where(wide == k, lane_sum(rows_of(tp[k], b) * rows_of(q, b)), line)
            inner[b * tile:b * tile + n_s, :] = line
        away = jnp.dot(member_t[...], inner[...], precision=lax.Precision.HIGHEST, preferred_element_type=F32)
        acc = None
        for k in range(n_k):
            for near in range(3):
                weight = -away[near * tile:near * tile + n_s, k:k + 1]
                if near == 1:
                    weight = weight + lane_sum(tl[k] * q)
                term = wk[near, k] * weight
                acc = term if acc is None else acc + term
        return jnp.sum(acc, axis=0, keepdims=True)

    odd = lax.rem(crs, 2) == 1

    def multiply(ju, n):
        row = lax.broadcasted_iota(jnp.int32, ju.shape, 0)
        acc = jnp.zeros((n_s, n_row), F32)
        for s in range(n_s):
            u = jnp.where(row == s, ju, 0.0).astype(jnp.bfloat16)
            acc = acc + lax.dot_general(u, ops[s], (((1,), (1,)), ((), ())), preferred_element_type=F32)
        blank = jnp.zeros((n_s, 2 * LANES - n_row), F32)
        lined = jnp.where(odd, jnp.concatenate([blank, acc], axis=1), jnp.concatenate([acc, blank], axis=1))
        for half in range(2):
            piece = rows_of(lined, half)
            qmsg[n, half] = piece
            qrecv[n, n_crs - 1, half] = piece
        spread(qmsg.at[n], qrecv.at[n], q_send.at[n], q_recv.at[n], "crs", crs, n_crs)
        arrivals(qrecv.at[n], q_send.at[n], q_recv.at[n], "crs", crs, n_crs).wait_recv()
        for pair in range(n_crs // 2):
            even, uneven = slot_of(2 * pair, crs, n_crs), slot_of(2 * pair + 1, crs, n_crs)
            at = 3 * pair * LANES
            qv[:, at:at + LANES] = qrecv[n, even, 0]
            qv[:, at + LANES:at + 2 * LANES] = jnp.where(wide < LANES // 2, qrecv[n, even, 1], qrecv[n, uneven, 0])
            qv[:, at + 2 * LANES:at + 3 * LANES] = qrecv[n, uneven, 1]

    for one in fetch[:5]:
        one.wait()
    col = jnp.zeros((1, n_col), F32)
    for s in range(n_s):
        for k in range(n_k):
            keep = jnp.where(k < modes[s], load[s * n_k + k], 0.0)
            line = factor[s * n_k + k:s * n_k + k + 1, :]
            wk[1, k, s:s + 1, :] = line
            col = col + line * keep
    fetch[5].wait()
    for s in range(n_s):
        for k in range(n_k):
            keep = jnp.where(k < modes[s], 1.0, 0.0).astype(F32)
            tk[k, s:s + 1, :] = traces[s, k:k + 1, :] * keep
    for k in range(n_k):
        for b in range(n_b):
            planes[k, pl.ds(b, n_s, stride=n_b), :] = rows_of(tk[k], b)
    mine = jnp.where(wide == tile + lax.broadcasted_iota(jnp.int32, (n_s, LANES), 0), 1.0, 0.0).astype(F32)
    for b in range(n_b):
        planes[n_k, pl.ds(b, n_s, stride=n_b), :] = mine

    def pick_planes(n, carry):
        for side in range(2):
            for m in range(8):
                at = jnp.maximum(sends[side, n * 8 + m], 0)
                for k in range(n_k + 1):
                    tmsg[side, k, pl.ds(n * 8 + m, 1), :] = planes[k, pl.ds(at, 1), :]
        return carry
    lax.fori_loop(0, slots // 8, pick_planes, 0)
    fetch[6].wait()
    jump_start(rhs, 0)

    pl.semaphore_wait(barrier, n_sub - 1 + n_crs - 1)

    sub_start(0, col, ())
    factor_copies = both((factor, factor), wrecv, w_send, w_recv)
    trace_copies = both((tmsg.at[0], tmsg.at[1]), trecv, t_send, t_recv)
    for one in factor_copies + jump_copies(0) + trace_copies:
        one.start()

    for one in factor_copies:
        one.wait_recv()
    for side in range(2):
        for s in range(n_s):
            for k in range(n_k):
                wk[2 * side, k, s:s + 1, :] = wrecv[side, s * n_k + k:s * n_k + k + 1, :]
    jres[...] = jump_end(rhs[...], 0)
    res[...] = rhs[...]
    member[...] = jnp.zeros(member.shape, F32)
    inner[...] = jnp.zeros(inner.shape, F32)
    col, _ = sub_end(0)
    back(0, col)

    for one in trace_copies:
        one.wait_recv()
    for side in range(2):
        for k in range(n_k):
            planes[k, pl.ds(n_local + side * slots, slots), :] = trecv[side, k]
        planes[n_k, pl.ds(n_local + side * slots, slots), :] = pltpu.roll(
            trecv[side, n_k], LANES - tile if side == 0 else tile, 1)

    def pair_planes(s, carry):
        for b in range(n_b):
            code = partner[s, b]
            at = jnp.maximum(code, 0)
            keep = jnp.where(code < 0, 0.0, 1.0).astype(F32)
            for k in range(n_k + 1):
                mates[k, pl.ds(s * n_b + b, 1), :] = planes[k, pl.ds(at, 1), :] * keep
        return carry
    lax.fori_loop(0, n_s, pair_planes, 0)
    for b in range(n_b):
        hot = mates[n_k, pl.ds(b, n_s, stride=n_b), :]
        member[b * tile:b * tile + n_s, :] = hot
        linked = lane_sum(hot)
        for k in range(n_k):
            tp[k, :, b * LANES:(b + 1) * LANES] = mates[k, pl.ds(b, n_s, stride=n_b), :]
            tl[k, :, b * LANES:(b + 1) * LANES] = rows_of(tk[k], b) * linked
    turned = jnp.concatenate([jnp.transpose(member[0:LANES, :]), jnp.transpose(
        jnp.concatenate([member[LANES:, :], jnp.zeros((2 * LANES - member.shape[0], LANES), F32)], axis=0))], axis=1)
    member_t[...] = turned[:3 * tile, :]
    start_col = restrict_col(jres[...])

    mix, _ = back_end(0)
    expand(mix)
    fetch[7].wait()
    out_m[...] = lift[...]
    multiply(2.0 * lift[...], 0)
    sub_start(1, start_col - 2.0 * adjoint_col(qv[...]), ())
    jump_start(qv, 1)
    for one in jump_copies(1):
        one.start()
    applied = jump_end(qv[...], 1)
    r = res[...] - applied
    res[...] = r
    jres[...] = jres[...] - 2.0 * applied
    square_start(0, r)
    col, _ = sub_end(1)
    back(1, col)
    mix, folded = back_end(1)
    expand(mix)
    rw = square_end(0) - folded
    way[...] = res[...] - lift[...]
    jway[...] = jres[...] - 2.0 * lift[...]
    for turn in range(ITERATIONS):
        final = turn == ITERATIONS - 1
        multiply(jway[...], 1 + turn)
        q = qv[...]
        sub_start(2 + turn, 2.0 * adjoint_col(q), (total(jway[...] * q),))
        jump_start(qv, 2 + turn)
        for one in jump_copies(2 + turn):
            one.start()
        applied = jump_end(qv[...], 2 + turn)
        qv[...] = applied
        change, tail = sub_end(2 + turn)
        alpha = rw / tail[:, 0:1]
        col = col - alpha * change
        back(2 + turn, col)
        r = res[...] - alpha * qv[...]
        res[...] = r
        if not final:
            square_start(1 + turn, r)
            jres[...] = jres[...] - 2.0 * alpha * qv[...]
        out_m[...] = out_m[...] + alpha * way[...]
        mix, folded = back_end(2 + turn)
        expand(mix)
        if final:
            out_p[...] = res[...] - lift[...]
        else:
            following = square_end(1 + turn) - folded
            beta = following / rw
            jway[...] = jres[...] - 2.0 * lift[...] + beta * jway[...]
            way[...] = res[...] - lift[...] + beta * way[...]
            rw = following

    for n in range(ITERATIONS + 2):
        arrivals(crecv.at[n], c_send.at[n], c_recv.at[n], "sub", sub, n_sub).wait_send()
        arrivals(xrecv.at[n], x_send.at[n], x_recv.at[n], "crs", crs, n_crs).wait_send()
    for n in range(ITERATIONS + 1):
        arrivals(qrecv.at[n], q_send.at[n], q_recv.at[n], "crs", crs, n_crs).wait_send()
    for n in range(ITERATIONS):
        arrivals(rrecv.at[n], r_send.at[n], r_recv.at[n], "sub", sub, n_sub).wait_send()
    for j in range(ITERATIONS + 2):
        for one in jump_copies(j):
            one.wait_send()
    for one in factor_copies + trace_copies:
        one.wait_send()


def local(n_sub, n_crs, ops, traces, factor, partner, sends, modes, rhs, load):
    n_s, n_row, order = ops.shape
    n_k = traces.shape[1]
    n_col = factor.shape[1]
    slots = sends.shape[1]
    n_b = order // LANES
    n_local = n_s * n_b
    n_c, n_q, n_j, n_r = ITERATIONS + 2, ITERATIONS + 1, ITERATIONS + 2, ITERATIONS
    far = pl.BlockSpec(memory_space=pltpu.HBM)
    vmem = pl.BlockSpec(memory_space=pltpu.VMEM)
    dma = pltpu.SemaphoreType.DMA
    vector = (n_s, order)
    small = (partner, sends, modes, load)
    large = (ops, traces, factor, rhs)
    shapes = [
        (n_k, n_s, order),
        (n_k, n_s, order),
        (n_k, n_s, order),
        (3, n_k, n_s, n_col),
        (n_k + 1, n_local + 2 * slots, LANES),
        (n_k + 1, n_local, LANES),
        (n_b * 16, LANES),
        (48, 2 * LANES),
        (2 * LANES, LANES),
        (n_local + 2 * slots, LANES),
        (n_local, LANES),
        vector,
        vector,
        vector,
        vector,
        vector,
        vector,
        (n_c, 4, LANES),
        (n_c, n_sub, 4, LANES),
        (n_c, 8, LANES),
        (n_c, n_crs, 8, LANES),
        (n_q, 2, n_s, LANES),
        (n_q, n_crs, 2, n_s, LANES),
        (n_j, 2, slots, LANES),
        (n_j, 2, slots, LANES),
        (2, n_k + 1, slots, LANES),
        (2, n_k + 1, slots, LANES),
        (2,) + factor.shape,
        (n_r, 1, LANES),
        (n_r, n_sub, 1, LANES),
    ]
    sems = [(8,), (n_c,), (n_c,), (n_c,), (n_c,), (n_q,), (n_q,), (n_j, 2), (n_j, 2), (2,), (2,), (2,), (2,),
            (n_r,), (n_r,)]
    return pl.pallas_call(
        functools.partial(kernel, n_sub, n_crs),
        out_shape=(jax.ShapeDtypeStruct(vector, F32), jax.ShapeDtypeStruct(vector, F32)),
        in_specs=[far] * 8,
        out_specs=(vmem, vmem),
        scratch_shapes=(
            [pltpu.SMEM(a.shape, a.dtype) for a in small]
            + [pltpu.VMEM(a.shape, a.dtype) for a in large]
            + [pltpu.VMEM(a, F32) for a in shapes]
            + [dma(a) for a in sems]
        ),
        compiler_params=pltpu.CompilerParams(
            collective_id=0, has_side_effects=True, vmem_limit_bytes=67043328
        ),
    )(*small, *large)


def solution(mesh):
    return jax.shard_map(
        functools.partial(local, mesh.shape["sub"], mesh.shape["crs"]),
        mesh=mesh,
        in_specs=(
            P("sub", "crs", None),
            P("sub", None, None),
            P("sub", "crs"),
            P("sub", None),
            P("sub", None),
            P("sub"),
            P("sub", None),
            P("sub"),
        ),
        out_specs=(P("sub", None), P("sub", None)),
        check_vma=False,
    )
```

time: 113 us -> 90.2 us (0.80)
  Pallas kernels: 105 us -> 86.3 us
  local copies, waits for them, and re-layouts: 6.81 us -> 3.08 us
    pallas_call x1, Pallas kernels: 105 us -> 86.3 us  [local(): pl.pallas_call(functools.partial(kernel, n_sub, n_crs), out_shape=(jax.Sh...]
    unnamed x16 -> x2, local copies, waits for them, and re-layouts: 6.81 us -> 3.08 us
where the time goes in v2:
time: 90.2 us; the launch traced here: 90 us
  Pallas kernels  86.3 us (96%)
  local copies, waits for them, and re-layouts  3.08 us (3%)
    pallas_call x1, Pallas kernels, local(): pl.pallas_call(functools.partial(kernel, n_sub, n_crs), out_shape=(jax.Sh...  86.3 us
    unnamed x2, local copies, waits for them, and re-layouts  3.08 us

profile of v2, /device:TPU:1, one launch (start us, length us, event | category | flops | bytes accessed | tf_op | source)
XLA Modules:
  0.0 90.0 jit_solution(4662085917537378890)
XLA Ops:
  0.6 86.3 %shard_map.95 = (f32[12,1536]{1,0:T(8,128)}, f32[12,1536]{1,0:T(8,128)}) custom-call(s32[12,12]{1,0:T(8,128)} %partner_in.1, s32[2,72]{1,0:T(2,128)} %sends_in.1, s32[12]{0:T(128)} %modes_in.1, f32[72]{0:T(128)} %load_in.1, bf16[12,192,1536]{2,1,0:T(8,128)(2,1)} %ops_in.1, f32[12,6,1536]{2,1,0:T(8,128)} %traces_in.1, f32[72,288]{1,0:T(8,128)} %factor_in.1, ...), custom_call_target="tpu_custom_call" | custom-call | tf_op jit(solution)/shard_map/pallas_call | solution.py:443
  87.0 1.5 %copy.12 = f32[12,1536]{1,0:T(8,128)} copy(f32[12,1536]{1,0:T(8,128)} %get-tuple-element.4) | data formatting | bytes 147456
  88.5 1.5 %copy.13 = f32[12,1536]{1,0:T(8,128)} copy(f32[12,1536]{1,0:T(8,128)} %get-tuple-element.5) | data formatting | bytes 147456

commit v3 on v2

v3 whole, which is shorter than its diff:
```python
import functools

import jax
import jax.numpy as jnp
from jax import lax
from jax.experimental import pallas as pl
from jax.experimental.pallas import tpu as pltpu
from jax.sharding import PartitionSpec as P

ITERATIONS = 2
LANES = 128
F32 = jnp.float32


def lane_sum(a):
    return jnp.sum(a, axis=1, keepdims=True)


def total(a):
    return jnp.sum(lane_sum(a), axis=0, keepdims=True)


def kernel(
    n_sub, n_crs,
    partner_in, sends_in, modes_in, load_in, ops_in, traces_in, factor_in, rhs_in,
    out_m, out_p,
    partner, sends, modes, load, ops, traces, factor, rhs,
    tl, tp, wk, planes, mates, member, member_t, inner, mates_x, gather, mate, lift, qv, applied, res, jres, way, jway, mult,
    rounded, cols, lines, col_now, extra, rw, chunk,
    cmsg, crecv, xmsg, xrecv, qmsg, qrecv, hmsg, hrecv, tmsg, trecv, wrecv, rmsg, rrecv,
    in_sem, c_send, c_recv, x_send, x_recv, q_send, q_recv, h_send, h_recv, t_send, t_recv, w_send, w_recv,
    r_send, r_recv,
):
    n_s, n_row, order = ops.shape
    n_b = order // LANES
    n_local = n_s * n_b
    n_k = tl.shape[0]
    last = ITERATIONS + 1
    n_col = factor.shape[1]
    slots = sends.shape[1]
    tile = 16
    sub = lax.axis_index("sub")
    crs = lax.axis_index("crs")

    pairs = ((partner_in, partner), (sends_in, sends), (modes_in, modes), (load_in, load),
             (factor_in, factor), (traces_in, traces), (rhs_in, rhs), (ops_in, ops))
    fetch = [pltpu.make_async_copy(a, b, in_sem.at[n]) for n, (a, b) in enumerate(pairs)]
    for one in fetch:
        one.start()

    barrier = pltpu.get_barrier_semaphore()

    def greet(axis, me, count):
        def one(t, carry):
            pl.semaphore_signal(
                barrier, inc=1, device_id={axis: lax.rem(me + t, count)},
                device_id_type=pl.DeviceIdType.MESH,
            )
            return carry
        lax.fori_loop(1, count, one, 0)

    greet("sub", sub, n_sub)
    greet("crs", crs, n_crs)

    def copy(src, dst, send, recv, where):
        return pltpu.make_async_remote_copy(
            src_ref=src, dst_ref=dst, send_sem=send, recv_sem=recv,
            device_id=where, device_id_type=pl.DeviceIdType.MESH,
        )

    def spread(msg, slots_ref, send, recv, axis, me, count):
        def one(t, carry):
            copy(msg, slots_ref.at[t - 1], send, recv, {axis: lax.rem(me + t, count)}).start()
            return carry
        lax.fori_loop(1, count, one, 0)

    def arrivals(slots_ref, send, recv, axis, me, count):
        whole = slots_ref.at[pl.ds(0, count - 1)]
        return copy(whole, whole, send, recv, {axis: lax.rem(me + 1, count)})

    def slot_of(who, me, count):
        return lax.rem(me - who - 1 + count, count)

    before, after = lax.rem(sub + n_sub - 1, n_sub), lax.rem(sub + 1, n_sub)

    def both(msg, recv_ref, send, recv):
        return [copy(msg[0], recv_ref.at[1], send.at[0], recv.at[1], {"sub": before}),
                copy(msg[1], recv_ref.at[0], send.at[1], recv.at[0], {"sub": after})]

    def rows_of(v, b):
        return v[:, b * LANES:(b + 1) * LANES]

    def jump_start(v, j):
        for b in range(n_b):
            gather[pl.ds(b, n_s, stride=n_b), :] = v[b]

        def pick(n, carry):
            for side in range(2):
                for m in range(8):
                    at = jnp.maximum(sends[side, n * 8 + m], 0)
                    hmsg[j, side, pl.ds(n * 8 + m, 1), :] = gather[pl.ds(at, 1), :]
            return carry
        lax.fori_loop(0, slots // 8, pick, 0)

    def jump_copies(j):
        return both((hmsg.at[j, 0], hmsg.at[j, 1]), hrecv.at[j], h_send.at[j], h_recv.at[j])

    def jump_end(v, out, j):
        one, two = jump_copies(j)
        one.wait_recv()
        two.wait_recv()
        for side in range(2):
            gather[pl.ds(n_local + side * slots, slots), :] = hrecv[j, side]

        def pair(s, carry):
            for b in range(n_b):
                code = partner[s, b]
                at = jnp.where(code < 0, s * n_b + b, code)
                mate[pl.ds(s * n_b + b, 1), :] = gather[pl.ds(at, 1), :]
            return carry
        lax.fori_loop(0, n_s, pair, 0)
        for b in range(n_b):
            out[b] = v[b] - mate[pl.ds(b, n_s, stride=n_b), :]

    lane = lax.broadcasted_iota(jnp.int32, (1, LANES), 1)
    wide = lax.broadcasted_iota(jnp.int32, (n_s, LANES), 1)

    def sub_start(n, col, scalars):
        rows = []
        for at in range(3):
            piece = col[:, at * LANES:min((at + 1) * LANES, n_col)]
            if piece.shape[1] < LANES:
                piece = jnp.concatenate([piece, jnp.zeros((1, LANES - piece.shape[1]), F32)], axis=1)
            rows.append(piece)
        last = jnp.zeros((1, LANES), F32)
        for at, value in enumerate(scalars):
            last = jnp.where(lane == at, value, last)
        msg = jnp.concatenate(rows + [last], axis=0)
        cmsg[n] = msg
        spread(cmsg.at[n], crecv.at[n], c_send.at[n], c_recv.at[n], "sub", sub, n_sub)

    def tree(got):
        while len(got) > 1:
            got = [got[i] + got[i + 1] for i in range(0, len(got), 2)]
        return got[0]

    def sub_end(n):
        arrivals(crecv.at[n], c_send.at[n], c_recv.at[n], "sub", sub, n_sub).wait_recv()
        tot = tree([crecv[n, at] for at in range(n_sub - 1)] + [cmsg[n]])
        col = jnp.concatenate([tot[0:1], tot[1:2], tot[2:3, :n_col - 2 * LANES]], axis=1)
        return col, tot[3:4]

    def square_start(n, v):
        line = jnp.where(lane == 0, total(jnp.sum(v * v, axis=0)), 0.0)
        rmsg[n] = line
        spread(rmsg.at[n], rrecv.at[n], r_send.at[n], r_recv.at[n], "sub", sub, n_sub)

    def square_end(n):
        arrivals(rrecv.at[n], r_send.at[n], r_recv.at[n], "sub", sub, n_sub).wait_recv()
        return tree([rrecv[n, at] for at in range(n_sub - 1)] + [rmsg[n]])[:, 0:1]

    n_x = 3 * n_k
    fold_at = 2 * n_x + 4

    def back(n, col):
        mix = jnp.zeros((n_s, LANES), F32)
        for near in range(3):
            for k in range(n_k):
                mix = jnp.where(wide == near * n_k + k, lane_sum(wk[near, k] * col), mix)
        low = jnp.concatenate([mix[8:n_s], jnp.zeros((16 - n_s, LANES), F32)], axis=0)
        msg = mix[0:8] + pltpu.roll(low, n_x, 1)
        at = (lax.broadcasted_iota(jnp.int32, (8, LANES), 1) == fold_at) & (
            lax.broadcasted_iota(jnp.int32, (8, LANES), 0) == 0)
        msg = jnp.where(at, lane_sum(col * col), msg)
        xmsg[n] = msg
        xrecv[n, n_crs - 1] = msg
        spread(xmsg.at[n], xrecv.at[n], x_send.at[n], x_recv.at[n], "crs", crs, n_crs)

    def back_end(n):
        arrivals(xrecv.at[n], x_send.at[n], x_recv.at[n], "crs", crs, n_crs).wait_recv()
        tot = tree([xrecv[n, slot_of(who, crs, n_crs)] for who in range(n_crs)])
        low = pltpu.roll(tot, LANES - n_x, 1)
        return jnp.concatenate([tot, low[:n_s - 8]], axis=0), tot[0:1, fold_at:fold_at + 1]

    def expand(mix):
        spare = jnp.zeros((tile - n_s, LANES), F32)
        rows = []
        for near in range(3):
            rows += [pltpu.roll(mix, LANES - near * n_k, 1) if near else mix, spare]
        rows.append(jnp.zeros((LANES - 3 * tile, LANES), F32))
        far = jnp.dot(member[...].reshape(n_b * tile, LANES), jnp.concatenate(rows, axis=0),
                      precision=lax.Precision.HIGHEST, preferred_element_type=F32)
        mates_x[...] = far.reshape(n_b, tile, LANES)
        own = [jnp.broadcast_to(mix[:, n_k + k:n_k + k + 1], (n_s, LANES)) for k in range(n_k)]

        def step(g, carry):
            for i in range(4):
                b = g * 4 + i
                theirs = mates_x[b][:n_s]
                acc = None
                for k in range(n_k):
                    term = tl[k, b] * own[k] - tp[k, b] * theirs[:, k:k + 1]
                    acc = term if acc is None else acc + term
                lift[b] = acc
            return carry
        lax.fori_loop(0, n_b // 4, step, 0)

    def restrict_col(jv):
        acc = None
        for k in range(n_k):
            term = wk[1, k] * lane_sum(jnp.sum(tl[k] * jv, axis=0))
            acc = term if acc is None else acc + term
        return jnp.sum(acc, axis=0, keepdims=True)

    def adjoint_col():
        def step(g, own):
            own = list(own)
            for i in range(4):
                b = g * 4 + i
                q = qv[b]
                line = jnp.zeros((n_s, LANES), F32)
                for k in range(n_k):
                    line = jnp.where(wide == k, lane_sum(tp[k, b] * q), line)
                    own[k] = own[k] + tl[k, b] * q
                inner[b, 0:n_s, :] = line
            return tuple(own)
        own = lax.fori_loop(0, n_b // 4, step, tuple(jnp.zeros((n_s, LANES), F32) for k in range(n_k)))
        away = jnp.dot(member_t[...], inner[...].reshape(2 * LANES, LANES), precision=lax.Precision.HIGHEST,
                       preferred_element_type=F32)
        acc = None
        for k in range(n_k):
            for near in range(3):
                weight = -away[near * tile:near * tile + n_s, k:k + 1]
                if near == 1:
                    weight = weight + lane_sum(own[k])
                term = wk[near, k] * weight
                acc = term if acc is None else acc + term
        return jnp.sum(acc, axis=0, keepdims=True)

    odd = lax.rem(crs, 2) == 1
    n_mx = n_s // 3
    here = lax.broadcasted_iota(jnp.int32, (n_row, LANES), 1)

    def multiply(n):
        rounded[...] = jway[...].astype(jnp.bfloat16).astype(F32)

        def step(i, carry):
            line = jnp.concatenate([rounded[b, pl.ds(i, 1), :] for b in range(n_b)], axis=1)
            out = lax.dot_general(jnp.broadcast_to(line, (16, order)).astype(jnp.bfloat16), ops[i],
                                  (((1,), (1,)), ((), ())), preferred_element_type=F32)
            lines[0, pl.ds(i, 1), :] = out[0:1, :LANES]
            lines[1, pl.ds(i, 1), :] = jnp.concatenate(
                [out[0:1, LANES:], jnp.zeros((1, 2 * LANES - n_row), F32)], axis=1)
            for j in range(2):
                s = n_mx + 2 * i + j
                acc = None
                for b in range(n_b):
                    term = ops[s, :, b * LANES:(b + 1) * LANES].astype(F32) * rounded[b, pl.ds(s, 1), :]
                    acc = term if acc is None else acc + term
                cols[0:n_row, :] = jnp.where(here == s, lane_sum(acc), cols[0:n_row, :])
            return carry
        lax.fori_loop(0, n_mx, step, 0)
        top = lax.broadcasted_iota(jnp.int32, (n_s, LANES), 0) < n_mx
        acc = jnp.concatenate([
            jnp.where(top, lines[half], jnp.transpose(cols[half * LANES:(half + 1) * LANES, :])[:n_s])
            for half in range(2)], axis=1)[:, :n_row]
        blank = jnp.zeros((n_s, 2 * LANES - n_row), F32)
        lined = jnp.where(odd, jnp.concatenate([blank, acc], axis=1), jnp.concatenate([acc, blank], axis=1))
        for half in range(2):
            piece = rows_of(lined, half)
            qmsg[n, half] = piece
            qrecv[n, n_crs - 1, half] = piece
        spread(qmsg.at[n], qrecv.at[n], q_send.at[n], q_recv.at[n], "crs", crs, n_crs)
        arrivals(qrecv.at[n], q_send.at[n], q_recv.at[n], "crs", crs, n_crs).wait_recv()
        for pair in range(n_crs // 2):
            even, uneven = slot_of(2 * pair, crs, n_crs), slot_of(2 * pair + 1, crs, n_crs)
            qv[3 * pair] = qrecv[n, even, 0]
            qv[3 * pair + 1] = jnp.where(wide < LANES // 2, qrecv[n, even, 1], qrecv[n, uneven, 0])
            qv[3 * pair + 2] = qrecv[n, uneven, 1]

    for one in fetch[:5]:
        one.wait()
    def by_mode(near, rows_in):
        for at in range(3):
            piece = rows_in[:, at * LANES:min((at + 1) * LANES, n_col)]
            chunk[at, :, 0:piece.shape[1]] = piece
        for k in range(n_k):
            for at in range(3):
                wide_at = min((at + 1) * LANES, n_col) - at * LANES
                wk[near, k, :, at * LANES:at * LANES + wide_at] = chunk[at, pl.ds(k, n_s, stride=n_k), :][:, :wide_at]
    by_mode(1, factor)
    depth = lax.broadcasted_iota(jnp.int32, (n_s, LANES), 0)

    def take_load(s, acc):
        line = jnp.zeros((1, LANES), F32)
        for k in range(n_k):
            line = jnp.where(lane == k, jnp.where(k < modes[s], load[s * n_k + k], 0.0), line)
        return jnp.where(depth == s, line, acc)
    loaded = lax.fori_loop(0, n_s, take_load, jnp.zeros((n_s, LANES), F32))
    acc = None
    for k in range(n_k):
        term = wk[1, k] * loaded[:, k:k + 1]
        acc = term if acc is None else acc + term
    first_col = jnp.sum(acc, axis=0, keepdims=True)
    fetch[5].wait()

    def place(s, carry):
        for k in range(n_k):
            keep = jnp.where(k < modes[s], 1.0, 0.0).astype(F32)
            for b in range(n_b):
                planes[k, pl.ds(s * n_b + b, 1), :] = traces[s, k:k + 1, b * LANES:(b + 1) * LANES] * keep
        return carry
    lax.fori_loop(0, n_s, place, 0)
    mine = jnp.where(wide == tile + depth, 1.0, 0.0).astype(F32)
    for b in range(n_b):
        planes[n_k, pl.ds(b, n_s, stride=n_b), :] = mine

    def pick_planes(n, carry):
        for side in range(2):
            for m in range(4):
                at = jnp.maximum(sends[side, n * 4 + m], 0)
                for k in range(n_k + 1):
                    tmsg[side, k, pl.ds(n * 4 + m, 1), :] = planes[k, pl.ds(at, 1), :]
        return carry
    lax.fori_loop(0, slots // 4, pick_planes, 0)
    fetch[6].wait()
    for b in range(n_b):
        res[b] = rhs[:, b * LANES:(b + 1) * LANES]
    jump_start(res, 0)

    pl.semaphore_wait(barrier, n_sub - 1 + n_crs - 1)

    sub_start(0, -first_col, ())
    factor_copies = both((factor, factor), wrecv, w_send, w_recv)
    trace_copies = both((tmsg.at[0], tmsg.at[1]), trecv, t_send, t_recv)
    for one in factor_copies + jump_copies(0) + trace_copies:
        one.start()

    for ref in (member, inner, cols, mult, way, jway, applied, col_now, extra, rw):
        ref[...] = jnp.zeros(ref.shape, F32)
    for one in factor_copies:
        one.wait_recv()
    for side in range(2):
        by_mode(2 * side, wrecv.at[side])
    jump_end(res, jres, 0)
    fetch[7].wait()

    def take_traces():
        for one in trace_copies:
            one.wait_recv()
        for side in range(2):
            for k in range(n_k):
                planes[k, pl.ds(n_local + side * slots, slots), :] = trecv[side, k]
            planes[n_k, pl.ds(n_local + side * slots, slots), :] = pltpu.roll(
                trecv[side, n_k], LANES - tile if side == 0 else tile, 1)

        def pair_planes(s, carry):
            for b in range(n_b):
                code = partner[s, b]
                at = jnp.maximum(code, 0)
                keep = jnp.where(code < 0, 0.0, 1.0).astype(F32)
                for k in range(n_k + 1):
                    mates[k, pl.ds(s * n_b + b, 1), :] = planes[k, pl.ds(at, 1), :] * keep
            return carry
        lax.fori_loop(0, n_s, pair_planes, 0)
        for b in range(n_b):
            hot = mates[n_k, pl.ds(b, n_s, stride=n_b), :]
            member[b, 0:n_s, :] = hot
            linked = lane_sum(hot)
            for k in range(n_k):
                tp[k, b] = mates[k, pl.ds(b, n_s, stride=n_b), :]
                tl[k, b] = planes[k, pl.ds(b, n_s, stride=n_b), :] * linked
        flat = member[...].reshape(n_b * tile, LANES)
        turned = jnp.concatenate([jnp.transpose(flat[:LANES]), jnp.transpose(jnp.concatenate(
            [flat[LANES:], jnp.zeros((2 * LANES - n_b * tile, LANES), F32)], axis=0))], axis=1)
        member_t[...] = turned[:3 * tile, :]
        extra[...] = restrict_col(jres[...])

    def phase(n, carry):
        fresh = n <= 1
        change, tail = sub_end(n)
        alpha = jnp.where(fresh, jnp.ones((1, 1), F32), rw[:, 0:1] / jnp.where(fresh, jnp.ones((1, 1), F32), tail[:, 0:1]))
        col = jnp.where(fresh, jnp.zeros(change.shape, F32), col_now[...]) - alpha * change
        col_now[...] = col
        back(n, col)
        r = res[...] - alpha * applied[...]
        res[...] = r

        @pl.when((n >= 1) & (n < last))
        def _():
            square_start(n - 1, res[...])
            jres[...] = jres[...] - 2.0 * alpha * applied[...]

        @pl.when(n == 0)
        def _():
            take_traces()

        @pl.when(n > 1)
        def _():
            mult[...] = mult[...] + alpha * way[...]
        mix, folded = back_end(n)
        expand(mix)

        @pl.when(n == 0)
        def _():
            mult[...] = lift[...]
            jway[...] = 2.0 * lift[...]

        @pl.when((n >= 1) & (n < last))
        def _():
            following = square_end(n - 1) - folded
            beta = jnp.where(fresh, jnp.zeros((1, 1), F32), following / jnp.where(fresh, jnp.ones((1, 1), F32), rw[:, 0:1]))
            jway[...] = jres[...] - 2.0 * lift[...] + jnp.where(fresh, 0.0, beta * jway[...])
            way[...] = res[...] - lift[...] + beta * way[...]
            rw[...] = jnp.broadcast_to(following, rw.shape)

        @pl.when(n < last)
        def _():
            multiply(n)
            message = 2.0 * adjoint_col() - extra[...]
            sub_start(n + 1, message, (total(jnp.sum(jway[...] * qv[...], axis=0)),))
            jump_start(qv, n + 1)
            for one in jump_copies(n + 1):
                one.start()
            extra[...] = jnp.zeros(extra.shape, F32)
            jump_end(qv, applied, n + 1)
        return carry
    lax.fori_loop(0, last + 1, phase, 0)

    for b in range(n_b):
        out_m[:, b * LANES:(b + 1) * LANES] = mult[b]
        out_p[:, b * LANES:(b + 1) * LANES] = res[b] - lift[b]

    for n in range(ITERATIONS + 2):
        arrivals(crecv.at[n], c_send.at[n], c_recv.at[n], "sub", sub, n_sub).wait_send()
        arrivals(xrecv.at[n], x_send.at[n], x_recv.at[n], "crs", crs, n_crs).wait_send()
    for n in range(ITERATIONS + 1):
        arrivals(qrecv.at[n], q_send.at[n], q_recv.at[n], "crs", crs, n_crs).wait_send()
    for n in range(ITERATIONS):
        arrivals(rrecv.at[n], r_send.at[n], r_recv.at[n], "sub", sub, n_sub).wait_send()
    for j in range(ITERATIONS + 2):
        for one in jump_copies(j):
            one.wait_send()
    for one in factor_copies + trace_copies:
        one.wait_send()


def local(n_sub, n_crs, ops, traces, factor, partner, sends, modes, rhs, load):
    n_s, n_row, order = ops.shape
    n_k = traces.shape[1]
    n_col = factor.shape[1]
    slots = sends.shape[1]
    n_b = order // LANES
    n_local = n_s * n_b
    n_c, n_q, n_j, n_r = ITERATIONS + 2, ITERATIONS + 1, ITERATIONS + 2, ITERATIONS
    far = pl.BlockSpec(memory_space=pltpu.HBM)
    vmem = pl.BlockSpec(memory_space=pltpu.VMEM)
    dma = pltpu.SemaphoreType.DMA
    vector = (n_b, n_s, LANES)
    small = (partner, sends, modes, load)
    large = (ops, traces, factor, rhs)
    shapes = [
        (n_k,) + vector,
        (n_k,) + vector,
        (3, n_k, n_s, n_col),
        (n_k + 1, n_local + 2 * slots, LANES),
        (n_k + 1, n_local, LANES),
        (n_b, 16, LANES),
        (48, 2 * LANES),
        (16, 16, LANES),
        (n_b, 16, LANES),
        (n_local + 2 * slots, LANES),
        (n_local, LANES),
        vector,
        vector,
        vector,
        vector,
        vector,
        vector,
        vector,
        vector,
        vector,
        (2 * LANES, LANES),
        (2, n_s, LANES),
        (1, n_col),
        (1, n_col),
        (1, LANES),
        (3, n_s * n_k, LANES),
        (n_c, 4, LANES),
        (n_c, n_sub - 1, 4, LANES),
        (n_c, 8, LANES),
        (n_c, n_crs, 8, LANES),
        (n_q, 2, n_s, LANES),
        (n_q, n_crs, 2, n_s, LANES),
        (n_j, 2, slots, LANES),
        (n_j, 2, slots, LANES),
        (2, n_k + 1, slots, LANES),
        (2, n_k + 1, slots, LANES),
        (2,) + factor.shape,
        (n_r, 1, LANES),
        (n_r, n_sub - 1, 1, LANES),
    ]
    sems = [(8,), (n_c,), (n_c,), (n_c,), (n_c,), (n_q,), (n_q,), (n_j, 2), (n_j, 2), (2,), (2,), (2,), (2,),
            (n_r,), (n_r,)]
    return pl.pallas_call(
        functools.partial(kernel, n_sub, n_crs),
        out_shape=(jax.ShapeDtypeStruct((n_s, order), F32), jax.ShapeDtypeStruct((n_s, order), F32)),
        in_specs=[far] * 8,
        out_specs=(vmem, vmem),
        scratch_shapes=(
            [pltpu.SMEM(a.shape, a.dtype) for a in small]
            + [pltpu.VMEM(a.shape, a.dtype) for a in large]
            + [pltpu.VMEM(a, F32) for a in shapes]
            + [dma(a) for a in sems]
        ),
        compiler_params=pltpu.CompilerParams(
            collective_id=0, has_side_effects=True, vmem_limit_bytes=40 * 1024 * 1024
        ),
    )(*[pltpu.with_memory_space_constraint(a, pltpu.HBM) for a in small + large])


def solution(mesh):
    return jax.shard_map(
        functools.partial(local, mesh.shape["sub"], mesh.shape["crs"]),
        mesh=mesh,
        in_specs=(
            P("sub", "crs", None),
            P("sub", None, None),
            P("sub", "crs"),
            P("sub", None),
            P("sub", None),
            P("sub"),
            P("sub", None),
            P("sub"),
        ),
        out_specs=(P("sub", None), P("sub", None)),
        check_vma=False,
    )
```

time: 90.2 us -> 83.7 us (0.928)
  Pallas kernels: 86.3 us -> 81.7 us
  local copies, waits for them, and re-layouts: 3.08 us -> 1.28 us
    pallas_call x1, Pallas kernels: 86.3 us -> 81.7 us  [local(): pl.pallas_call(functools.partial(kernel, n_sub, n_crs), out_shape=(jax.Sh...]
    unnamed x2, local copies, waits for them, and re-layouts: 3.08 us -> 1.28 us
where the time goes in v3:
time: 83.7 us; the launch traced here: 83.6 us
  Pallas kernels  81.7 us (98%)
  local copies, waits for them, and re-layouts  1.28 us (2%)
    pallas_call x1, Pallas kernels, local(): pl.pallas_call(functools.partial(kernel, n_sub, n_crs), out_shape=(jax.Sh...  81.7 us

profile of v3, /device:TPU:1, one launch (start us, length us, event | category | flops | bytes accessed | tf_op | source)
XLA Modules:
  0.0 83.6 jit_solution(1818697637800675110)
XLA Ops:
  0.6 81.7 %shard_map.95 = (f32[12,1536]{1,0:T(8,128)S(1)}, f32[12,1536]{1,0:T(8,128)S(1)}) custom-call(s32[12,12]{1,0:T(8,128)} %partner_in.1, s32[2,72]{1,0:T(2,128)} %sends_in.1, s32[12]{0:T(128)} %modes_in.1, f32[72]{0:T(128)} %load_in.1, bf16[12,192,1536]{2,1,0:T(8,128)(2,1)} %ops_in.1, f32[12,6,1536]{2,1,0:T(8,128)} %traces_in.1, f32[72,288]{1,0:T(8,128)} %factor_in.1, ...), custom_call_target="tpu_custom_call" | custom-call | tf_op jit(solution)/shard_map/pallas_call | solution.py:505
  82.3 0.6 copy.12
  83.0 0.6 copy.13

commit v4 on v3

--- a/solution.py
+++ b/solution.py
@@ -69,10 +69,10 @@
         )
 
     def spread(msg, slots_ref, send, recv, axis, me, count):
-        def one(t, carry):
+        def one(t):
             copy(msg, slots_ref.at[t - 1], send, recv, {axis: lax.rem(me + t, count)}).start()
-            return carry
-        lax.fori_loop(1, count, one, 0)
+        for t in range(1, count):
+            one(t)
 
     def arrivals(slots_ref, send, recv, axis, me, count):
         whole = slots_ref.at[pl.ds(0, count - 1)]
@@ -203,7 +203,8 @@
                     acc = term if acc is None else acc + term
                 lift[b] = acc
             return carry
-        lax.fori_loop(0, n_b // 4, step, 0)
+        for g in range(n_b // 4):
+            step(g, 0)
 
     def restrict_col(jv):
         acc = None
@@ -224,7 +225,9 @@
                     own[k] = own[k] + tl[k, b] * q
                 inner[b, 0:n_s, :] = line
             return tuple(own)
-        own = lax.fori_loop(0, n_b // 4, step, tuple(jnp.zeros((n_s, LANES), F32) for k in range(n_k)))
+        own = tuple(jnp.zeros((n_s, LANES), F32) for k in range(n_k))
+        for g in range(n_b // 4):
+            own = step(g, own)
         away = jnp.dot(member_t[...], inner[...].reshape(2 * LANES, LANES), precision=lax.Precision.HIGHEST,
                        preferred_element_type=F32)
         acc = None
@@ -259,7 +262,8 @@
                     acc = term if acc is None else acc + term
                 cols[0:n_row, :] = jnp.where(here == s, lane_sum(acc), cols[0:n_row, :])
             return carry
-        lax.fori_loop(0, n_mx, step, 0)
+        for i in range(n_mx):
+            step(i, 0)
         top = lax.broadcasted_iota(jnp.int32, (n_s, LANES), 0) < n_mx
         acc = jnp.concatenate([
             jnp.where(top, lines[half], jnp.transpose(cols[half * LANES:(half + 1) * LANES, :])[:n_s])
@@ -383,8 +387,10 @@
         col = jnp.where(fresh, jnp.zeros(change.shape, F32), col_now[...]) - alpha * change
         col_now[...] = col
         back(n, col)
-        r = res[...] - alpha * applied[...]
-        res[...] = r
+        @pl.when(n >= 1)
+        def _():
+            jump_end(qv, applied, n)
+        res[...] = res[...] - alpha * applied[...]
 
         @pl.when((n >= 1) & (n < last))
         def _():
@@ -423,7 +429,6 @@
             for one in jump_copies(n + 1):
                 one.start()
             extra[...] = jnp.zeros(extra.shape, F32)
-            jump_end(qv, applied, n + 1)
         return carry
     lax.fori_loop(0, last + 1, phase, 0)
 

time: 83.7 us -> 82 us (0.980)
  Pallas kernels: 81.7 us -> 80 us
    pallas_call x1, Pallas kernels: 81.7 us -> 80 us  [local(): pl.pallas_call(functools.partial(kernel, n_sub, n_crs), out_shape=(jax.Sh...]
where the time goes in v4:
time: 82 us; the launch traced here: 81.9 us
  Pallas kernels  80 us (98%)
  local copies, waits for them, and re-layouts  1.28 us (2%)
    pallas_call x1, Pallas kernels, local(): pl.pallas_call(functools.partial(kernel, n_sub, n_crs), out_shape=(jax.Sh...  80 us

profile of v4, /device:TPU:1, one launch (start us, length us, event | category | flops | bytes accessed | tf_op | source)
XLA Modules:
  0.0 81.9 jit_solution(3163181918943963555)
XLA Ops:
  0.6 80.0 %shard_map.95 = (f32[12,1536]{1,0:T(8,128)S(1)}, f32[12,1536]{1,0:T(8,128)S(1)}) custom-call(s32[12,12]{1,0:T(8,128)} %partner_in.1, s32[2,72]{1,0:T(2,128)} %sends_in.1, s32[12]{0:T(128)} %modes_in.1, f32[72]{0:T(128)} %load_in.1, bf16[12,192,1536]{2,1,0:T(8,128)(2,1)} %ops_in.1, f32[12,6,1536]{2,1,0:T(8,128)} %traces_in.1, f32[72,288]{1,0:T(8,128)} %factor_in.1, ...), custom_call_target="tpu_custom_call" | custom-call | tf_op jit(solution)/shard_map/pallas_call | solution.py:510
  80.6 0.6 copy.12
  81.3 0.6 copy.13
